TPU v7x, 768 devices: a whole 4x8x12 slice. The times are simulated.
768 devices in a mesh: slab: 12 (over z), inner: 64 (over x, y, core).
Axes of the slice: x: 4, y: 8, z: 12, core: 2. Of those that a mesh axis runs over, the one named last changes fastest.
Arguments:
- matrix_blocks: bfloat16 [12288, 27, 64, 64], P(('slab', 'inner')), may hold values from -6 to 6
- prolong: bfloat16 [12288, 64, 64], P(('slab', 'inner')), may hold values from -0.75 to 0.75
- columns: int32 [12288, 27], P(('slab', 'inner')), may hold values from 0 to 12287, as said below
- partial_slot: int32 [12288, 27], P(('slab', 'inner')), may hold values from 0 to 47
- into_slot: int32 [768, 48], P(('slab', 'inner')), may hold values from 0 to 31
Outputs:
- coarse: float32 [24576, 4096], P(('slab', 'inner'))
Inputs may be any that keep to these rules, and one draw needn't show every extreme that they name: `columns`: A slab's block rows form a periodic grid of 2 x 64 x (8) blocks: row s * 1024 + q * 16 + x * 8 + z sits at (x, q, z). Entry [i, 0] is i itself; entries 1 to 26 are the 26 grid neighbours of i (offsets -1, 0, 1 in each dimension, modulo the grid), in an order drawn for each row.
All inputs are finite; a program needn't handle non-finite values.
Results may differ from a plain program's by a relative error of at most 0.0029.
Values may be sent and summed in bfloat16 or wider, within the bound.
No kernel may reach another device: no remote copies, remote signals or barrier semaphores. Data moves between devices by JAX's collectives and lax.ppermute only.
A program may use at most 128 MiB of HBM per device.

v0:
```python
import jax
import jax.numpy as jnp
from jax import lax
from jax.sharding import PartitionSpec as P

NBR = 27
BUF = 16
SLOTS = 32


def padded(value, sides, width):
    for axis, dim in sides:
        devices, length = (lax.axis_size(axis), value.shape[dim])
        up = [(i, (i + 1) % devices) for i in range(devices)]
        down = [(j, i) for i, j in up]
        last = lax.slice_in_dim(value, length - width, length, axis=dim)
        leading = lax.slice_in_dim(value, 0, width, axis=dim)
        before = lax.ppermute(last, axis, up)
        after = lax.ppermute(leading, axis, down)
        value = jnp.concatenate([before, value, after], axis=dim)
    return value


def shifted(value, axis, steps):
    count = lax.axis_size(axis)
    pairs = [(source, (source + steps) % count) for source in range(count)]
    return lax.ppermute(value, axis, pairs)


def per_device(matrix_blocks, prolong, columns, partial_slot, into_slot):
    row_count = prolong.shape[0]
    block_width = prolong.shape[1]
    group_size = lax.axis_size("inner")
    local_cols = columns.reshape(-1) % (row_count * group_size)
    widened = padded(prolong, (("inner", 0),), row_count)
    own_layer = lax.axis_index("inner")
    col_layer = local_cols // row_count
    col_row = local_cols % row_count
    place = (col_layer - own_layer + 1) % group_size * row_count + col_row
    picked = jnp.take(widened, place, axis=0)
    right_mat = picked.reshape(row_count, NBR, block_width, block_width)
    applied = jnp.einsum(
        "rkab,rkbc->rkac", matrix_blocks, right_mat, preferred_element_type=jnp.float32
    ).astype(jnp.bfloat16)
    contrib = jnp.einsum("rab,rkac->rkbc", prolong, applied, preferred_element_type=jnp.float32)
    chooser = (
        partial_slot[:, :, None] == jnp.arange(3 * BUF, dtype=jnp.int32)[None, None, :]
    ).astype(jnp.float32)
    summed = jnp.einsum("rkm,rkbc->mbc", chooser, contrib, precision=lax.Precision.HIGHEST)
    partial_value = summed.reshape(3 * BUF, block_width * block_width)
    from_left = shifted(partial_value[2 * BUF :], "slab", 1)
    from_right = shifted(partial_value[:BUF], "slab", -1)
    incoming = jnp.concatenate([from_left, partial_value[BUF : 2 * BUF], from_right], axis=0)
    owner_pick = (into_slot[0][None, :] == jnp.arange(SLOTS, dtype=jnp.int32)[:, None]).astype(
        jnp.float32
    )
    return jnp.dot(owner_pick, incoming, precision=lax.Precision.HIGHEST)


def solution(mesh):
    return jax.shard_map(
        per_device,
        mesh=mesh,
        in_specs=(
            P(("slab", "inner"), None, None, None),
            P(("slab", "inner"), None, None),
            P(("slab", "inner"), None),
            P(("slab", "inner"), None),
            P(("slab", "inner"), None),
        ),
        out_specs=P(("slab", "inner"), None),
        check_vma=False,
    )
```

profile of v0, /device:TPU:6, one launch (start us, length us, event | category | flops | bytes accessed | tf_op | source)
XLA Modules:
  0.0 94.8 jit_solution(16559937588523429261)
XLA Ops:
  0.0 5.1 %collective-permute-start.1 = (bf16[16,64,64]{2,1,0:T(8,128)(2,1)}, bf16[16,64,64]{2,1,0:T(8,128)(2,1)S(1)}, u32[]{:S(2)}, u32[]{:S(2)}) collective-permute-start(bf16[16,64,64]{2,1,0:T(8,128)(2,1)} %param.6), channel_id=1, source_target_pairs={{1,0},{2,1},{3,2},{4,3},{5,4},{6,5},{7,6},{8,7},{9,8},{10,9},{11,1... | collective-permute-start | bytes 393224 | tf_op jit(solution)/shard_map/ppermute | solution.py:19
  5.1 1.9 %collective-permute-start = (bf16[16,64,64]{2,1,0:T(8,128)(2,1)}, bf16[16,64,64]{2,1,0:T(8,128)(2,1)S(1)}, u32[]{:S(2)}, u32[]{:S(2)}) collective-permute-start(bf16[16,64,64]{2,1,0:T(8,128)(2,1)} %param.6), channel_id=1, source_target_pairs={{0,1},{1,2},{2,3},{3,4},{4,5},{5,6},{6,7},{7,8},{8,9},{9,10},{10,1... | collective-permute-start | bytes 393224 | tf_op jit(solution)/shard_map/ppermute | solution.py:18
  7.0 0.8 reshape.187
  7.8 0.7 compare_and_fusion
  8.6 0.7 collective-permute-done.1
  9.3 5.8 %collective-permute-done = bf16[16,64,64]{2,1,0:T(8,128)(2,1)S(1)} collective-permute-done((bf16[16,64,64]{2,1,0:T(8,128)(2,1)}, bf16[16,64,64]{2,1,0:T(8,128)(2,1)S(1)}, u32[]{:S(2)}, u32[]{:S(2)}) %collective-permute-start) | collective-permute-done | bytes 131104 | tf_op jit(solution)/shard_map/ppermute | solution.py:18
  15.1 1.1 %pad_maximum_fusion = bf16[48,64,64]{2,1,0:T(8,128)(2,1)S(1)} fusion(bf16[16,64,64]{2,1,0:T(8,128)(2,1)S(1)} %collective-permute-done.1, bf16[16,64,64]{2,1,0:T(8,128)(2,1)} %param.6, bf16[16,64,64]{2,1,0:T(8,128)(2,1)S(1)} %collective-permute-done), kind=kLoop, calls=%fused_computation.11 | loop fusion | flops 393216 | bytes 786432 | tf_op jit(solution)/shard_map/concatenate | solution.py:20
  16.2 0.0 copy-start
  16.2 13.3 %gather_fusion = bf16[432,64,64]{2,1,0:T(8,128)(2,1)} fusion(bf16[48,64,64]{2,1,0:T(8,128)(2,1)S(1)} %pad_maximum_fusion, s32[1024]{0:T(1024)S(1)} %pad_clamp_fusion), kind=kCustom, calls=%fused_computation | custom fusion | bytes 7079616 | tf_op jit(solution)/shard_map/jit(_take)/gather | solution.py:40
  29.6 14.1 %fusion.2 = f32[16,27,64,64]{3,2,1,0:T(8,128)} fusion(bf16[16,27,64,64]{3,2,1,0:T(8,128)(2,1)} %param.5, bf16[16,27,64,64]{3,2,1,0:T(8,128)(2,1)} %bitcast.23, pred[16,27]{1,0:T(8,128)(4,1)S(1)} %compare_and_fusion, bf16[16,64,64]{2,1,0:T(8,128)(2,1)S(1)} %copy-done), kind=kOutput, calls=%fused_computation.3 | convolution fusion | flops 456523776 | bytes 14287280 | tf_op jit(solution)/shard_map/rab,rkac->rkbc/dot_general | solution.py:45
  43.7 18.4 %copy.10 = f32[16,27,64,64]{2,1,0,3:T(8,128)} copy(f32[16,27,64,64]{3,2,1,0:T(8,128)} %fusion.2) | data formatting | bytes 14155776 | tf_op jit(solution)/shard_map/rab,rkac->rkbc/dot_general | solution.py:45
  62.1 10.2 %fusion.15 = f32[48,64,64]{2,0,1:T(8,128)S(1)} fusion(f32[16,27,64,64]{2,1,0,3:T(8,128)} %copy.10, s32[16,27]{1,0:T(8,128)S(1)} %copy-done.1), kind=kOutput, calls=%fused_computation.10 | convolution fusion | flops 1019236608 | bytes 7866048 | tf_op jit(solution)/shard_map/rkm,rkbc->mbc/dot_general | solution.py:49
  72.3 0.1 fusion.43
  72.5 0.2 copy.6
  72.7 0.2 slice.19
  72.8 4.3 %collective-permute-start.2 = (f32[16,4096]{1,0:T(8,128)S(1)}, f32[16,4096]{1,0:T(8,128)S(1)}, u32[]{:S(2)}, u32[]{:S(2)}) collective-permute-start(f32[16,4096]{1,0:T(8,128)S(1)} %slice.19), channel_id=1, source_target_pairs={{0,64},{64,128},{128,192},{192,256},{256,320},{320,384},{384,448},... | collective-permute-start | bytes 786440 | tf_op jit(solution)/shard_map/ppermute | solution.py:27
  77.1 0.2 copy.8
  77.3 0.2 slice.23
  77.5 12.2 %collective-permute-start.3 = (f32[16,4096]{1,0:T(8,128)S(1)}, f32[16,4096]{1,0:T(8,128)S(1)}, u32[]{:S(2)}, u32[]{:S(2)}) collective-permute-start(f32[16,4096]{1,0:T(8,128)S(1)} %slice.23), channel_id=1, source_target_pairs={{0,704},{64,0},{128,64},{192,128},{256,192},{320,256},{384,320},{4... | collective-permute-start | bytes 786440 | tf_op jit(solution)/shard_map/ppermute | solution.py:27
  89.7 0.2 copy.7
  89.9 0.2 slice.21
  90.1 1.7 %collective-permute-done.2 = f32[16,4096]{1,0:T(8,128)S(1)} collective-permute-done((f32[16,4096]{1,0:T(8,128)S(1)}, f32[16,4096]{1,0:T(8,128)S(1)}, u32[]{:S(2)}, u32[]{:S(2)}) %collective-permute-start.2) | collective-permute-done | bytes 262176 | tf_op jit(solution)/shard_map/ppermute | solution.py:27
  91.7 1.8 %collective-permute-done.3 = f32[16,4096]{1,0:T(8,128)S(1)} collective-permute-done((f32[16,4096]{1,0:T(8,128)S(1)}, f32[16,4096]{1,0:T(8,128)S(1)}, u32[]{:S(2)}, u32[]{:S(2)}) %collective-permute-start.3) | collective-permute-done | bytes 262176 | tf_op jit(solution)/shard_map/ppermute | solution.py:27
  93.6 1.2 %fusion.18 = f32[32,4096]{1,0:T(8,128)} fusion(f32[16,4096]{1,0:T(8,128)S(1)} %collective-permute-done.3, f32[16,4096]{1,0:T(8,128)S(1)} %slice.21, f32[16,4096]{1,0:T(8,128)S(1)} %collective-permute-done.2, s32[48]{0:T(128)S(1)} %bitcast.25), kind=kOutput, calls=%fused_computation.12 | convolution fusion | flops 75892224 | bytes 1310912 | tf_op jit(solution)/shard_map/dot_general | solution.py:57
  (7 shorter events, 0.1 us)
Async XLA Ops:
  0.0 9.3 %collective-permute-start.1 = (bf16[16,64,64]{2,1,0:T(8,128)(2,1)}, bf16[16,64,64]{2,1,0:T(8,128)(2,1)S(1)}, u32[]{:S(2)}, u32[]{:S(2)}) collective-permute-start(bf16[16,64,64]{2,1,0:T(8,128)(2,1)} %param.6), channel_id=1, source_target_pairs={{1,0},{2,1},{3,2},{4,3},{5,4},{6,5},{7,6},{8,7},{9,8},{10,9},{11,1... | collective-permute-start | bytes 393224 | tf_op jit(solution)/shard_map/ppermute | solution.py:19
  5.1 10.0 %collective-permute-start = (bf16[16,64,64]{2,1,0:T(8,128)(2,1)}, bf16[16,64,64]{2,1,0:T(8,128)(2,1)S(1)}, u32[]{:S(2)}, u32[]{:S(2)}) collective-permute-start(bf16[16,64,64]{2,1,0:T(8,128)(2,1)} %param.6), channel_id=1, source_target_pairs={{0,1},{1,2},{2,3},{3,4},{4,5},{5,6},{6,7},{7,8},{8,9},{9,10},{10,1... | collective-permute-start | bytes 393224 | tf_op jit(solution)/shard_map/ppermute | solution.py:18
  16.2 13.4 %copy-start = (bf16[16,64,64]{2,1,0:T(8,128)(2,1)S(1)}, bf16[16,64,64]{2,1,0:T(8,128)(2,1)}, u32[]{:S(2)}) copy-start(bf16[16,64,64]{2,1,0:T(8,128)(2,1)} %param.6) | copy-start | bytes 393220
  43.7 18.4 %copy-start.1 = (s32[16,27]{1,0:T(8,128)S(1)}, s32[16,27]{1,0:T(8,128)}, u32[]{:S(2)}) copy-start(s32[16,27]{1,0:T(8,128)} %param.8) | copy-start | bytes 5188
  72.3 21.2 %copy-start.2 = (s32[1,48]{1,0:T(1,128)S(1)}, s32[1,48]{1,0:T(1,128)}, u32[]{:S(2)}) copy-start(s32[1,48]{1,0:T(1,128)} %param.9) | copy-start | bytes 580
  72.8 18.9 %collective-permute-start.2 = (f32[16,4096]{1,0:T(8,128)S(1)}, f32[16,4096]{1,0:T(8,128)S(1)}, u32[]{:S(2)}, u32[]{:S(2)}) collective-permute-start(f32[16,4096]{1,0:T(8,128)S(1)} %slice.19), channel_id=1, source_target_pairs={{0,64},{64,128},{128,192},{192,256},{256,320},{320,384},{384,448},... | collective-permute-start | bytes 786440 | tf_op jit(solution)/shard_map/ppermute | solution.py:27
  77.5 16.1 %collective-permute-start.3 = (f32[16,4096]{1,0:T(8,128)S(1)}, f32[16,4096]{1,0:T(8,128)S(1)}, u32[]{:S(2)}, u32[]{:S(2)}) collective-permute-start(f32[16,4096]{1,0:T(8,128)S(1)} %slice.23), channel_id=1, source_target_pairs={{0,704},{64,0},{128,64},{192,128},{256,192},{320,256},{384,320},{4... | collective-permute-start | bytes 786440 | tf_op jit(solution)/shard_map/ppermute | solution.py:27
where the time goes:
time: 95.4 us; the launch traced here: 94.8 us
  local copies, waits for them, and re-layouts  33.7 us (35%)
  matrix products  25.6 us (27%)
  starting transfers between devices  23.5 us (25%)
  waiting for transfers between devices  9.99 us (10%)
  other arithmetic  1.9 us (2%)
    dot_general x1, local copies, waits for them, and re-layouts, per_device(): jnp.einsum('rab,rkac->rkbc', prolong, applied, preferred_element_type=jnp...  18.4 us
    ppermute x2, starting transfers between devices, shifted(): return lax.ppermute(value, axis, pairs)  16.5 us
    dot_general x1, matrix products, per_device(): jnp.einsum('rab,rkac->rkbc', prolong, applied, preferred_element_type=jnp...  14.1 us
    gather x1, local copies, waits for them, and re-layouts, per_device(): picked = jnp.take(widened, place, axis=0)  13.3 us
    dot_general x1, matrix products, per_device(): jnp.einsum('rkm,rkbc->mbc', chooser, contrib, precision=lax.Precision.HIG...  10.2 us
    ppermute x1, waiting for transfers between devices, padded(): before = lax.ppermute(last, axis, up)  5.83 us
    ppermute x1, starting transfers between devices, padded(): after = lax.ppermute(leading, axis, down)  5.07 us
    ppermute x2, waiting for transfers between devices, shifted(): return lax.ppermute(value, axis, pairs)  3.5 us
  transfers between devices with their start and end apart: 4, of which 4 were waited for; matrix products, arithmetic and copies ran while one was open for 2% of the time, Pallas kernels for 0%

commit v1 on v0

v1 whole, which is shorter than its diff:
```python
import jax
import jax.numpy as jnp
from jax import lax
from jax.experimental import pallas as pl
from jax.experimental.pallas import tpu as pltpu
from jax.sharding import PartitionSpec as P

BUF = 16
SLOTS = 32


def shifted(value, axis, steps):
    count = lax.axis_size(axis)
    pairs = [(source, (source + steps) % count) for source in range(count)]
    return lax.ppermute(value, axis, pairs)


def triple_kernel(layer_ref, cols, slots, before, own, after, blocks, out, wide):
    rows, per_row = cols.shape
    layers = layer_ref[1]
    wide[:rows] = before[...]
    wide[rows : 2 * rows] = own[...]
    wide[2 * rows :] = after[...]
    out[...] = jnp.zeros_like(out)

    def row(i, carry):
        left = own[i].T
        for k in range(per_row):
            col = cols[i, k]
            layer = lax.rem(lax.div(col, rows) - layer_ref[0] + layers, layers)
            place = layer * rows + lax.rem(col, rows)
            applied = jnp.dot(blocks[i, k], wide[place], preferred_element_type=jnp.float32)
            contrib = jnp.dot(left, applied.astype(jnp.bfloat16), preferred_element_type=jnp.float32)
            slot = slots[i, k]
            out[slot] = out[slot] + contrib
        return carry

    lax.fori_loop(0, rows, row, 0)


def per_device(matrix_blocks, prolong, columns, partial_slot, into_slot):
    rows, width = prolong.shape[:2]
    layers = lax.axis_size("inner")
    before = shifted(prolong, "inner", 1)
    after = shifted(prolong, "inner", -1)
    first = lax.rem(lax.axis_index("inner") + layers - 1, layers)
    base = first + lax.axis_index("slab") * layers
    layer_info = jnp.stack([base, jnp.int32(layers)]).astype(jnp.int32)
    smem = pl.BlockSpec(memory_space=pltpu.SMEM)
    vmem = pl.BlockSpec(memory_space=pltpu.VMEM)
    partial_value = pl.pallas_call(
        triple_kernel,
        out_shape=jax.ShapeDtypeStruct((3 * BUF, width, width), jnp.float32),
        in_specs=[smem, smem, smem, vmem, vmem, vmem, vmem],
        out_specs=vmem,
        scratch_shapes=[pltpu.VMEM((3 * rows, width, width), jnp.bfloat16)],
        compiler_params=pltpu.CompilerParams(vmem_limit_bytes=24 << 20),
        name="triple",
    )(layer_info, columns, partial_slot, before, prolong, after, matrix_blocks)
    partial_value = partial_value.reshape(3 * BUF, width * width)
    from_left = shifted(partial_value[2 * BUF :].astype(jnp.bfloat16), "slab", 1)
    from_right = shifted(partial_value[:BUF].astype(jnp.bfloat16), "slab", -1)
    picks = into_slot[0][None, :] == jnp.arange(SLOTS, dtype=jnp.int32)[:, None]
    kept = jnp.dot(
        picks[:, BUF : 2 * BUF].astype(jnp.float32),
        partial_value[BUF : 2 * BUF],
        precision=lax.Precision.HIGHEST,
    )
    sides = jnp.concatenate([picks[:, :BUF], picks[:, 2 * BUF :]], axis=1).astype(jnp.bfloat16)
    arrived = jnp.concatenate([from_left, from_right], axis=0)
    return kept + jnp.dot(sides, arrived, preferred_element_type=jnp.float32)


def solution(mesh):
    return jax.shard_map(
        per_device,
        mesh=mesh,
        in_specs=(
            P(("slab", "inner"), None, None, None),
            P(("slab", "inner"), None, None),
            P(("slab", "inner"), None),
            P(("slab", "inner"), None),
            P(("slab", "inner"), None),
        ),
        out_specs=P(("slab", "inner"), None),
        check_vma=False,
    )
```

time: 95.4 us -> 49.1 us (0.51)
  the two profiles are of different devices: /device:TPU:6 before, /device:TPU:29 now
where the time goes in v1:
time: 49.1 us; the launch traced here: 48.8 us
  starting transfers between devices  23.1 us (47%)
  Pallas kernels  8.93 us (18%)
  waiting for transfers between devices  8.05 us (16%)
  local copies, waits for them, and re-layouts  6.24 us (13%)
  matrix products  1.5 us (3%)
  other arithmetic  0.87 us (2%)
    ppermute x4, starting transfers between devices, shifted(): return lax.ppermute(value, axis, pairs)  23.1 us
    pallas_call x1, Pallas kernels, per_device(): pl.pallas_call(triple_kernel, out_shape=jax.ShapeDtypeStruct((3 * BUF, wi...  8.93 us
    ppermute x4, waiting for transfers between devices, shifted(): return lax.ppermute(value, axis, pairs)  8.05 us
    unnamed x8, local copies, waits for them, and re-layouts  5.35 us
    dot_general x1, matrix products, per_device(): jnp.dot(picks[:, BUF:2 * BUF].astype(jnp.float32), partial_value[BUF:2 *...  1.23 us
  transfers between devices with their start and end apart: 4, of which 3 were waited for; matrix products, arithmetic and copies ran while one was open for 3% of the time, Pallas kernels for 0%

profile of v1, /device:TPU:29, one launch (start us, length us, event | category | flops | bytes accessed | tf_op | source)
XLA Modules:
  0.0 48.8 jit_solution(11091204754302078623)
XLA Ops:
  0.0 5.0 %collective-permute-start = (bf16[16,64,64]{2,1,0:T(8,128)(2,1)}, bf16[16,64,64]{2,1,0:T(8,128)(2,1)S(1)}, u32[]{:S(2)}, u32[]{:S(2)}) collective-permute-start(bf16[16,64,64]{2,1,0:T(8,128)(2,1)} %own.1), channel_id=1, source_target_pairs={{0,1},{1,2},{2,3},{3,4},{4,5},{5,6},{6,7},{7,8},{8,9},{9,10},{10,1... | collective-permute-start | bytes 393224 | tf_op jit(solution)/shard_map/ppermute | solution.py:15
  5.0 1.9 %collective-permute-start.1 = (bf16[16,64,64]{2,1,0:T(8,128)(2,1)}, bf16[16,64,64]{2,1,0:T(8,128)(2,1)S(1)}, u32[]{:S(2)}, u32[]{:S(2)}) collective-permute-start(bf16[16,64,64]{2,1,0:T(8,128)(2,1)} %own.1), channel_id=1, source_target_pairs={{0,63},{1,0},{2,1},{3,2},{4,3},{5,4},{6,5},{7,6},{8,7},{9,8},{10,9... | collective-permute-start | bytes 393224 | tf_op jit(solution)/shard_map/ppermute | solution.py:15
  6.9 0.7 %iota_compare_fusion = pred[32,48]{1,0:T(32,128)(4,1)S(1)} fusion(s32[48]{0:T(128)} %bitcast.3), kind=kLoop, calls=%fused_computation.5 | loop fusion | flops 1536 | bytes 1728 | tf_op jit(solution)/shard_map/eq | solution.py:63
  7.6 0.1 pad_add_fusion.layer_ref
  7.6 0.9 %collective-permute-done.before = bf16[16,64,64]{2,1,0:T(8,128)(2,1)S(1)} collective-permute-done((bf16[16,64,64]{2,1,0:T(8,128)(2,1)}, bf16[16,64,64]{2,1,0:T(8,128)(2,1)S(1)}, u32[]{:S(2)}, u32[]{:S(2)}) %collective-permute-start) | collective-permute-done | bytes 131104 | tf_op jit(solution)/shard_map/ppermute | solution.py:15
  8.6 5.5 %collective-permute-done.1.after = bf16[16,64,64]{2,1,0:T(8,128)(2,1)S(1)} collective-permute-done((bf16[16,64,64]{2,1,0:T(8,128)(2,1)}, bf16[16,64,64]{2,1,0:T(8,128)(2,1)S(1)}, u32[]{:S(2)}, u32[]{:S(2)}) %collective-permute-start.1) | collective-permute-done | bytes 131104 | tf_op jit(solution)/shard_map/ppermute | solution.py:15
  14.1 0.0 copy-start
  14.1 3.0 %copy-done = bf16[16,27,64,64]{3,2,1,0:T(8,128)(2,1)S(1)} copy-done((bf16[16,27,64,64]{3,2,1,0:T(8,128)(2,1)S(1)}, bf16[16,27,64,64]{3,2,1,0:T(8,128)(2,1)}, u32[]{:S(2)}) %copy-start) | copy-done | bytes 3538968
  17.1 0.0 copy-start.1
  17.1 0.9 %copy-done.1 = bf16[16,64,64]{2,1,0:T(8,128)(2,1)S(1)} copy-done((bf16[16,64,64]{2,1,0:T(8,128)(2,1)S(1)}, bf16[16,64,64]{2,1,0:T(8,128)(2,1)}, u32[]{:S(2)}) %copy-start.1) | copy-done | bytes 131096
  18.1 0.7 %copy-done.2 = s32[16,27]{1,0:T(8,128)S(1)} copy-done((s32[16,27]{1,0:T(8,128)S(1)}, s32[16,27]{1,0:T(8,128)}, u32[]{:S(2)}) %copy-start.2) | copy-done | bytes 1752
  18.7 0.7 %copy-done.3 = s32[16,27]{1,0:T(8,128)S(1)} copy-done((s32[16,27]{1,0:T(8,128)S(1)}, s32[16,27]{1,0:T(8,128)}, u32[]{:S(2)}) %copy-start.3) | copy-done | bytes 1752
  19.4 8.9 %triple.1 = f32[48,64,64]{2,1,0:T(8,128)S(1)} custom-call(s32[2]{0:T(128)S(1)} %pad_add_fusion.layer_ref, s32[16,27]{1,0:T(8,128)S(1)} %copy-done.2, s32[16,27]{1,0:T(8,128)S(1)} %copy-done.3, bf16[16,64,64]{2,1,0:T(8,128)(2,1)S(1)} %collective-permute-done.before, bf16[16,64,64]{2,1,0:T(8,128)(2,1)S(1)} %copy-done.1, ...), custom_call_target="tpu_custom_call" | custom-call | tf_op jit(solution)/shard_map/triple/pallas_call | solution.py:51
  28.4 0.1 convert.4
  28.6 0.3 convert_element_type.10
  28.8 4.0 %collective-permute-start.2 = (bf16[16,4096]{1,0:T(8,128)(2,1)S(1)}, bf16[16,4096]{1,0:T(8,128)(2,1)S(1)}, u32[]{:S(2)}, u32[]{:S(2)}) collective-permute-start(bf16[16,4096]{1,0:T(8,128)(2,1)S(1)} %convert_element_type.10), channel_id=1, source_target_pairs={{0,64},{64,128},{128,192},{192,256},{256,320},{320,384},{384,448},... | collective-permute-start | bytes 393224 | tf_op jit(solution)/shard_map/ppermute | solution.py:15
  32.8 0.3 convert_element_type.11
  33.1 12.2 %collective-permute-start.3 = (bf16[16,4096]{1,0:T(8,128)(2,1)S(1)}, bf16[16,4096]{1,0:T(8,128)(2,1)S(1)}, u32[]{:S(2)}, u32[]{:S(2)}) collective-permute-start(bf16[16,4096]{1,0:T(8,128)(2,1)S(1)} %convert_element_type.11), channel_id=1, source_target_pairs={{0,704},{64,0},{128,64},{192,128},{256,192},{320,256},{384,320},{4... | collective-permute-start | bytes 393224 | tf_op jit(solution)/shard_map/ppermute | solution.py:15
  45.4 0.1 fusion.11
  45.5 0.2 slice.27
  45.7 0.0 collective-permute-done.2
  45.7 1.6 %collective-permute-done.3 = bf16[16,4096]{1,0:T(8,128)(2,1)S(1)} collective-permute-done((bf16[16,4096]{1,0:T(8,128)(2,1)S(1)}, bf16[16,4096]{1,0:T(8,128)(2,1)S(1)}, u32[]{:S(2)}, u32[]{:S(2)}) %collective-permute-start.3) | collective-permute-done | bytes 131104 | tf_op jit(solution)/shard_map/ppermute | solution.py:15
  47.3 0.3 fusion
  47.6 1.2 %convolution_add_fusion = f32[32,4096]{1,0:T(8,128)} fusion(f32[32,4096]{1,0:T(8,128)S(1)} %fusion, f32[16,4096]{1,0:T(8,128)S(1)} %slice.27, pred[32,48]{1,0:T(32,128)(4,1)S(1)} %iota_compare_fusion), kind=kOutput, calls=%fused_computation | convolution fusion | flops 25296896 | bytes 1312256 | tf_op jit(solution)/shard_map/dot_general | solution.py:64
  (4 shorter events, 0.1 us)
Async XLA Ops:
  0.0 8.6 %collective-permute-start = (bf16[16,64,64]{2,1,0:T(8,128)(2,1)}, bf16[16,64,64]{2,1,0:T(8,128)(2,1)S(1)}, u32[]{:S(2)}, u32[]{:S(2)}) collective-permute-start(bf16[16,64,64]{2,1,0:T(8,128)(2,1)} %own.1), channel_id=1, source_target_pairs={{0,1},{1,2},{2,3},{3,4},{4,5},{5,6},{6,7},{7,8},{8,9},{9,10},{10,1... | collective-permute-start | bytes 393224 | tf_op jit(solution)/shard_map/ppermute | solution.py:15
  5.0 9.1 %collective-permute-start.1 = (bf16[16,64,64]{2,1,0:T(8,128)(2,1)}, bf16[16,64,64]{2,1,0:T(8,128)(2,1)S(1)}, u32[]{:S(2)}, u32[]{:S(2)}) collective-permute-start(bf16[16,64,64]{2,1,0:T(8,128)(2,1)} %own.1), channel_id=1, source_target_pairs={{0,63},{1,0},{2,1},{3,2},{4,3},{5,4},{6,5},{7,6},{8,7},{9,8},{10,9... | collective-permute-start | bytes 393224 | tf_op jit(solution)/shard_map/ppermute | solution.py:15
  14.1 3.0 %copy-start = (bf16[16,27,64,64]{3,2,1,0:T(8,128)(2,1)S(1)}, bf16[16,27,64,64]{3,2,1,0:T(8,128)(2,1)}, u32[]{:S(2)}) copy-start(bf16[16,27,64,64]{3,2,1,0:T(8,128)(2,1)} %blocks.1) | copy-start | bytes 10616836
  17.1 0.9 %copy-start.1 = (bf16[16,64,64]{2,1,0:T(8,128)(2,1)S(1)}, bf16[16,64,64]{2,1,0:T(8,128)(2,1)}, u32[]{:S(2)}) copy-start(bf16[16,64,64]{2,1,0:T(8,128)(2,1)} %own.1) | copy-start | bytes 393220
  18.0 0.7 %copy-start.2 = (s32[16,27]{1,0:T(8,128)S(1)}, s32[16,27]{1,0:T(8,128)}, u32[]{:S(2)}) copy-start(s32[16,27]{1,0:T(8,128)} %cols.1) | copy-start | bytes 5188
  18.7 0.7 %copy-start.3 = (s32[16,27]{1,0:T(8,128)S(1)}, s32[16,27]{1,0:T(8,128)}, u32[]{:S(2)}) copy-start(s32[16,27]{1,0:T(8,128)} %slots.1) | copy-start | bytes 5188
  28.8 16.8 %collective-permute-start.2 = (bf16[16,4096]{1,0:T(8,128)(2,1)S(1)}, bf16[16,4096]{1,0:T(8,128)(2,1)S(1)}, u32[]{:S(2)}, u32[]{:S(2)}) collective-permute-start(bf16[16,4096]{1,0:T(8,128)(2,1)S(1)} %convert_element_type.10), channel_id=1, source_target_pairs={{0,64},{64,128},{128,192},{192,256},{256,320},{320,384},{384,448},... | collective-permute-start | bytes 393224 | tf_op jit(solution)/shard_map/ppermute | solution.py:15
  33.1 14.2 %collective-permute-start.3 = (bf16[16,4096]{1,0:T(8,128)(2,1)S(1)}, bf16[16,4096]{1,0:T(8,128)(2,1)S(1)}, u32[]{:S(2)}, u32[]{:S(2)}) collective-permute-start(bf16[16,4096]{1,0:T(8,128)(2,1)S(1)} %convert_element_type.11), channel_id=1, source_target_pairs={{0,704},{64,0},{128,64},{192,128},{256,192},{320,256},{384,320},{4... | collective-permute-start | bytes 393224 | tf_op jit(solution)/shard_map/ppermute | solution.py:15

commit v2 on v1

v2 whole, which is shorter than its diff:
```python
import jax
import jax.numpy as jnp
from jax import lax
from jax.experimental import pallas as pl
from jax.experimental.pallas import tpu as pltpu
from jax.sharding import PartitionSpec as P

W = 64
HALF = W // 2
LANES = 2 * W
NBR = 27
ROWS = 16
DEPTH = 8
BUF = 16
SLOTS = 32
LAYERS = 64
F32 = jnp.float32
BF = jnp.bfloat16
UNROLL_NEAR, UNROLL_FAR, UNROLL_STRIP = 8, 4, 8


def shifted(value, axis, steps):
    count = lax.axis_size(axis)
    pairs = [(source, (source + steps) % count) for source in range(count)]
    return lax.ppermute(value, axis, pairs)


def ordered(cols, slots):
    row = lax.broadcasted_iota(jnp.int32, cols.shape, 0)
    k = lax.broadcasted_iota(jnp.int32, cols.shape, 1)
    layer = (cols >> 4) & (LAYERS - 1)
    own = jnp.broadcast_to(layer[:, 0:1], cols.shape)
    d = (layer - own + 1) & (LAYERS - 1)
    other = ((cols >> 3) & 1) ^ (row >> 3)
    g = ((cols & 7) - (row & 7) + 1) & 7
    key = d * 6 + other * 3 + g
    value = (k * W + slots).astype(F32)
    table = jnp.zeros(cols.shape, F32)
    for d in range(3):
        for g in range(3):
            one = jnp.min(jnp.where(key == d * 6 + g, value, 1e9), axis=1, keepdims=True)
            two = key == d * 6 + 3 + g
            low = jnp.min(jnp.where(two, value, 1e9), axis=1, keepdims=True)
            high = jnp.max(jnp.where(two, value, -1.0), axis=1, keepdims=True)
            for u, found in enumerate((one, low, high)):
                table = jnp.where(k == d * 9 + u * 3 + g, found, table)
    return table.astype(jnp.int32)


def user(x, u, g, z):
    return (x if u == 0 else 1 - x) * DEPTH + ((z - g + 1) & (DEPTH - 1))


def add_to(acc, slot, value):
    spot = acc.at[pl.ds(pl.multiple_of(slot * HALF, HALF), HALF), :]
    spot[...] = spot[...] + value


def add_strip(left, strip, accs, slot_of, count):
    both = jnp.dot(left, strip, preferred_element_type=F32)
    low = lax.broadcasted_iota(jnp.int32, (HALF, LANES), 1) < W
    for e in range(0, count, 2):
        even = both[:HALF, W * e : W * e + LANES]
        odd = both[HALF:, W * e : W * e + LANES]
        add_to(accs[0], slot_of(e), jnp.where(low, even, pltpu.roll(odd, W, 1)))
        if e + 1 < count:
            add_to(accs[1], slot_of(e + 1), jnp.where(low, pltpu.roll(even, W, 1), odd))


def near_kernel(
    blocks, own, cols, slots, far, acc_a, acc_b, table, left,
    held, prolong, cols_v, slots_v, look, double, strip, sems, row_sems,
):
    small = [
        pltpu.make_async_copy(source, target, sems.at[n])
        for n, (source, target) in enumerate(((cols, cols_v), (slots, slots_v), (own, prolong)))
    ]
    for copy in small:
        copy.start()

    def fetches(z):
        return [
            pltpu.make_async_copy(blocks.at[i], held.at[i], row_sems.at[i]) for i in (z, z + DEPTH)
        ]

    for z in (7, 0, 1, 2, 3, 4, 5, 6):
        for copy in fetches(z):
            copy.start()
    acc_a[...] = jnp.zeros_like(acc_a)
    acc_b[...] = jnp.zeros_like(acc_b)
    small[0].wait()
    small[1].wait()
    table[...] = ordered(cols_v[...], slots_v[...])
    to_look = pltpu.make_async_copy(table, look, sems.at[3])
    to_look.start()
    small[2].wait()
    r = lax.broadcasted_iota(jnp.int32, (W, W), 0)
    c = lax.broadcasted_iota(jnp.int32, (W, W), 1)
    split = (c == (r % HALF) * 2 + r // HALF).astype(F32).astype(BF)
    for i in range(ROWS):
        p = prolong[i]
        double[i] = jnp.concatenate([p, p], axis=1)
        left[i] = lax.dot_general(
            split, p, (((1,), (1,)), ((), ())), preferred_element_type=F32
        ).astype(BF)
    to_look.wait()

    def block(i, d, u, g):
        return held[i, look[i, d * 9 + u * 3 + g] >> 6]

    def repack(z):
        for copy in fetches(z):
            copy.wait()
        for x in range(2):
            for u in range(3):
                for g in range(3):
                    at = (u * 3 + g) * W
                    side = LANES * (x if u == 0 else 1 - x)
                    i = x * DEPTH + z
                    pair = jnp.concatenate([block(i, 0, u, g), block(i, 2, u, g)], axis=1)
                    far[(z + g - 1) & (DEPTH - 1), at : at + W, side : side + LANES] = pair

    repack(7)
    repack(0)
    for z in range(DEPTH):
        if z < DEPTH - 2:
            repack(z + 1)
        for x in range(2):
            users = [(user(x, u, g, z), u, g) for u in range(3) for g in range(3)]
            stack = jnp.concatenate([block(i, 1, u, g) for i, u, g in users], axis=0)
            applied = jnp.dot(stack, double[x * DEPTH + z], preferred_element_type=F32).astype(BF)
            for e, (i, u, g) in enumerate(users):
                lane = W * (e % 2)
                strip[i, :, W * e : W * e + W] = applied[W * e : W * e + W, lane : lane + W]

    def finish(i, carry):
        add_strip(left[i], strip[i], (acc_a, acc_b), lambda e: look[i, 9 + e] & (W - 1), 9)
        return carry

    lax.fori_loop(0, ROWS, finish, 0, unroll=UNROLL_NEAR)


def far_kernel(
    table, blocks, near_a, near_b, left, before, after, up, mid, down,
    acc_a, acc_b, look, lows, highs, strip, sems,
):
    to_look = pltpu.make_async_copy(table, look, sems.at[0])
    to_look.start()
    none = jnp.zeros((W, W), BF)
    blank = jnp.zeros((W, LANES), BF)
    for j in range(ROWS):
        lows[j] = jnp.concatenate([before[j], none], axis=1)
        highs[j] = jnp.concatenate([none, after[j]], axis=1)
    part = acc_a.shape[0] // DEPTH

    def multiply(z, carry):
        rows = pl.ds(pl.multiple_of(z * part, part), part)
        acc_a[rows, :] = near_a[rows, :]
        acc_b[rows, :] = near_b[rows, :]
        four = [
            jnp.concatenate([lows[z], blank], axis=1),
            jnp.concatenate([highs[z], blank], axis=1),
            jnp.concatenate([blank, lows[DEPTH + z]], axis=1),
            jnp.concatenate([blank, highs[DEPTH + z]], axis=1),
        ]
        diagonal = jnp.concatenate(four, axis=0)
        applied = jnp.dot(blocks[z], diagonal, preferred_element_type=F32).astype(BF)
        for u in range(3):
            for g in range(3):
                at = (u * 3 + g) * W
                for x in range(2):
                    part_of = applied[at : at + W, LANES * x : LANES * x + LANES]
                    strip[user(x, u, g, z), :, 2 * at : 2 * at + LANES] = part_of
        return carry

    lax.fori_loop(0, DEPTH, multiply, 0, unroll=UNROLL_FAR)
    to_look.wait()

    def finish(i, carry):
        add_strip(
            left[i], strip[i], (acc_a, acc_b), lambda e: look[i, e // 2 + 18 * (e % 2)] & (W - 1), 18
        )
        return carry

    lax.fori_loop(0, ROWS, finish, 0, unroll=UNROLL_STRIP)
    for n, out in enumerate((down, mid, up)):
        rows = slice(n * BUF * HALF, (n + 1) * BUF * HALF)
        out[...] = (acc_a[rows, :] + acc_b[rows, :]).astype(out.dtype)


def gather_kernel(into, left, mid, right, out, acc):
    acc[...] = jnp.zeros_like(acc)
    for n, source in enumerate((left, mid, right)):
        for m in range(BUF):
            add_to(acc, into[0, n * BUF + m], source[HALF * m : HALF * m + HALF, :].astype(F32))
    out[...] = acc[...].reshape(out.shape)


def per_device(matrix_blocks, prolong, columns, partial_slot, into_slot):
    before = shifted(prolong, "inner", 1)
    after = shifted(prolong, "inner", -1)
    hbm = pl.BlockSpec(memory_space=pltpu.HBM)
    vmem = pl.BlockSpec(memory_space=pltpu.VMEM)
    smem = pl.BlockSpec(memory_space=pltpu.SMEM)
    sums = jax.ShapeDtypeStruct((3 * BUF * HALF, LANES), F32)
    third = (BUF * HALF, LANES)
    sent = jax.ShapeDtypeStruct(third, BF)
    table_v = pltpu.VMEM((ROWS, NBR), jnp.int32)
    table_s = pltpu.SMEM((ROWS, NBR), jnp.int32)
    wide = pltpu.VMEM((ROWS, W, LANES), BF)
    far, acc_a, acc_b, table, left = pl.pallas_call(
        near_kernel,
        out_shape=(
            jax.ShapeDtypeStruct((DEPTH, 9 * W, 4 * W), BF),
            sums,
            sums,
            jax.ShapeDtypeStruct((ROWS, NBR), jnp.int32),
            jax.ShapeDtypeStruct((ROWS, W, W), BF),
        ),
        in_specs=[hbm] * 4,
        out_specs=(vmem,) * 5,
        scratch_shapes=[
            pltpu.VMEM((ROWS, NBR, W, W), BF),
            pltpu.VMEM((ROWS, W, W), BF),
            table_v,
            table_v,
            table_s,
            wide,
            pltpu.VMEM((ROWS, W, 10 * W), BF),
            pltpu.SemaphoreType.DMA((4,)),
            pltpu.SemaphoreType.DMA((ROWS,)),
        ],
        compiler_params=pltpu.CompilerParams(vmem_limit_bytes=46 << 20),
        cost_estimate=pl.CostEstimate(flops=10**9, bytes_accessed=12 * 10**6, transcendentals=0),
        name="near",
    )(matrix_blocks, prolong, columns, partial_slot)
    up, mid, down = pl.pallas_call(
        far_kernel,
        out_shape=(sent, jax.ShapeDtypeStruct(third, F32), sent),
        in_specs=[vmem] * 7,
        out_specs=(vmem,) * 3,
        scratch_shapes=[
            pltpu.VMEM(sums.shape, F32),
            pltpu.VMEM(sums.shape, F32),
            table_s,
            wide,
            wide,
            pltpu.VMEM((ROWS, W, 18 * W), BF),
            pltpu.SemaphoreType.DMA((1,)),
        ],
        compiler_params=pltpu.CompilerParams(vmem_limit_bytes=24 << 20),
        name="far",
    )(table, far, acc_a, acc_b, left, before, after)
    from_left = shifted(up, "slab", 1)
    from_right = shifted(down, "slab", -1)
    return pl.pallas_call(
        gather_kernel,
        out_shape=jax.ShapeDtypeStruct((SLOTS, W * W), F32),
        in_specs=[smem, vmem, vmem, vmem],
        out_specs=vmem,
        scratch_shapes=[pltpu.VMEM((SLOTS * HALF, LANES), F32)],
        compiler_params=pltpu.CompilerParams(vmem_limit_bytes=16 << 20),
        name="gather",
    )(into_slot, from_left, mid, from_right)


def solution(mesh):
    return jax.shard_map(
        per_device,
        mesh=mesh,
        in_specs=(
            P(("slab", "inner"), None, None, None),
            P(("slab", "inner"), None, None),
            P(("slab", "inner"), None),
            P(("slab", "inner"), None),
            P(("slab", "inner"), None),
        ),
        out_specs=P(("slab", "inner"), None),
        check_vma=False,
    )
```

time: 49.1 us -> 39 us (0.79)
  the two profiles are of different devices: /device:TPU:29 before, /device:TPU:6 now
where the time goes in v2:
time: 39 us; the launch traced here: 38.7 us
  starting transfers between devices  23.5 us (60%)
  Pallas kernels  9.23 us (24%)
  waiting for transfers between devices  3.58 us (9%)
  local copies, waits for them, and re-layouts  2.34 us (6%)
    ppermute x4, starting transfers between devices, shifted(): return lax.ppermute(value, axis, pairs)  23.5 us
    pallas_call x1, Pallas kernels, per_device(): pl.pallas_call(near_kernel, out_shape=(jax.ShapeDtypeStruct((DEPTH, 9 * W...  4.64 us
    ppermute x4, waiting for transfers between devices, shifted(): return lax.ppermute(value, axis, pairs)  3.58 us
    pallas_call x1, Pallas kernels, per_device(): pl.pallas_call(far_kernel, out_shape=(sent, jax.ShapeDtypeStruct(third, F...  2.93 us
    unnamed x8, local copies, waits for them, and re-layouts  2.34 us
    pallas_call x1, Pallas kernels, per_device(): pl.pallas_call(gather_kernel, out_shape=jax.ShapeDtypeStruct((SLOTS, W *...  1.66 us
  transfers between devices with their start and end apart: 4, of which 3 were waited for; matrix products, arithmetic and copies ran while one was open for 0% of the time, Pallas kernels for 12%

profile of v2, /device:TPU:6, one launch (start us, length us, event | category | flops | bytes accessed | tf_op | source)
XLA Modules:
  0.0 38.7 jit_solution(14084322708573272925)
XLA Ops:
  0.0 5.1 %collective-permute-start.1 = (bf16[16,64,64]{2,1,0:T(8,128)(2,1)}, bf16[16,64,64]{2,1,0:T(8,128)(2,1)S(1)}, u32[]{:S(2)}, u32[]{:S(2)}) collective-permute-start(bf16[16,64,64]{2,1,0:T(8,128)(2,1)} %own.1), channel_id=1, source_target_pairs={{0,63},{1,0},{2,1},{3,2},{4,3},{5,4},{6,5},{7,6},{8,7},{9,8},{10,9... | collective-permute-start | bytes 393224 | tf_op jit(solution)/shard_map/ppermute | solution.py:25
  5.1 1.9 %collective-permute-start = (bf16[16,64,64]{2,1,0:T(8,128)(2,1)}, bf16[16,64,64]{2,1,0:T(8,128)(2,1)S(1)}, u32[]{:S(2)}, u32[]{:S(2)}) collective-permute-start(bf16[16,64,64]{2,1,0:T(8,128)(2,1)} %own.1), channel_id=1, source_target_pairs={{0,1},{1,2},{2,3},{3,4},{4,5},{5,6},{6,7},{7,8},{8,9},{9,10},{10,1... | collective-permute-start | bytes 393224 | tf_op jit(solution)/shard_map/ppermute | solution.py:25
  7.0 0.0 copy-start
  7.0 0.9 %copy-done = bf16[16,64,64]{2,1,0:T(8,128)(2,1)S(1)} copy-done((bf16[16,64,64]{2,1,0:T(8,128)(2,1)S(1)}, bf16[16,64,64]{2,1,0:T(8,128)(2,1)}, u32[]{:S(2)}) %copy-start) | copy-done | bytes 131096
  8.0 0.0 copy-start.1
  8.0 0.7 %copy-done.1 = s32[16,27]{1,0:T(8,128)S(1)} copy-done((s32[16,27]{1,0:T(8,128)S(1)}, s32[16,27]{1,0:T(8,128)}, u32[]{:S(2)}) %copy-start.1) | copy-done | bytes 1752
  8.7 0.0 copy-start.2
  8.7 0.7 %copy-done.2 = s32[16,27]{1,0:T(8,128)S(1)} copy-done((s32[16,27]{1,0:T(8,128)S(1)}, s32[16,27]{1,0:T(8,128)}, u32[]{:S(2)}) %copy-start.2) | copy-done | bytes 1752
  9.4 0.0 copy-start.3
  9.4 4.6 %near.1 = (bf16[8,576,256]{2,1,0:T(8,128)(2,1)S(1)}, f32[1536,128]{1,0:T(8,128)S(1)}, f32[1536,128]{1,0:T(8,128)S(1)}, s32[16,27]{1,0:T(8,128)S(1)}, bf16[16,64,64]{2,1,0:T(8,128)(2,1)S(1)}) custom-call(bf16[16,27,64,64]{3,2,1,0:T(8,128)(2,1)} %blocks.1, bf16[16,64,64]{2,1,0:T(8,128)(2,1)S(1)} %copy-done, s32[16,27]{1,0:T(8,128)S(1)} %copy-done.1, ...), custom_call_target="tpu_custom_call" | custom-call | flops 1000000000 | bytes 12000000 | tf_op jit(solution)/shard_map/near/pallas_call | solution.py:211
  14.0 0.0 collective-permute-done.1.after
  14.0 1.1 %collective-permute-done.before = bf16[16,64,64]{2,1,0:T(8,128)(2,1)S(1)} collective-permute-done((bf16[16,64,64]{2,1,0:T(8,128)(2,1)}, bf16[16,64,64]{2,1,0:T(8,128)(2,1)S(1)}, u32[]{:S(2)}, u32[]{:S(2)}) %collective-permute-start) | collective-permute-done | bytes 131104 | tf_op jit(solution)/shard_map/ppermute | solution.py:25
  15.1 2.9 %far.1 = (bf16[512,128]{1,0:T(8,128)(2,1)S(1)}, f32[512,128]{1,0:T(8,128)S(1)}, bf16[512,128]{1,0:T(8,128)(2,1)S(1)}) custom-call(s32[16,27]{1,0:T(8,128)S(1)} %get-tuple-element.13.table, bf16[8,576,256]{2,1,0:T(8,128)(2,1)S(1)} %get-tuple-element.14.blocks, f32[1536,128]{1,0:T(8,128)S(1)} %get-tuple-element.15.near_a, ...), custom_call_target="tpu_custom_call" | custom-call | tf_op jit(solution)/shard_map/far/pallas_call | solution.py:237
  18.0 4.3 %collective-permute-start.2 = (bf16[512,128]{1,0:T(8,128)(2,1)S(1)}, bf16[512,128]{1,0:T(8,128)(2,1)S(1)}, u32[]{:S(2)}, u32[]{:S(2)}) collective-permute-start(bf16[512,128]{1,0:T(8,128)(2,1)S(1)} %get-tuple-element.18), channel_id=1, source_target_pairs={{0,64},{64,128},{128,192},{192,256},{256,320},{320,384},{384,448},... | collective-permute-start | bytes 393224 | tf_op jit(solution)/shard_map/ppermute | solution.py:25
  22.3 12.2 %collective-permute-start.3 = (bf16[512,128]{1,0:T(8,128)(2,1)S(1)}, bf16[512,128]{1,0:T(8,128)(2,1)S(1)}, u32[]{:S(2)}, u32[]{:S(2)}) collective-permute-start(bf16[512,128]{1,0:T(8,128)(2,1)S(1)} %get-tuple-element.20), channel_id=1, source_target_pairs={{0,704},{64,0},{128,64},{192,128},{256,192},{320,256},{384,320},{4... | collective-permute-start | bytes 393224 | tf_op jit(solution)/shard_map/ppermute | solution.py:25
  34.6 1.0 %collective-permute-done.2.left = bf16[512,128]{1,0:T(8,128)(2,1)S(1)} collective-permute-done((bf16[512,128]{1,0:T(8,128)(2,1)S(1)}, bf16[512,128]{1,0:T(8,128)(2,1)S(1)}, u32[]{:S(2)}, u32[]{:S(2)}) %collective-permute-start.2) | collective-permute-done | bytes 131104 | tf_op jit(solution)/shard_map/ppermute | solution.py:25
  35.6 1.5 %collective-permute-done.3.right = bf16[512,128]{1,0:T(8,128)(2,1)S(1)} collective-permute-done((bf16[512,128]{1,0:T(8,128)(2,1)S(1)}, bf16[512,128]{1,0:T(8,128)(2,1)S(1)}, u32[]{:S(2)}, u32[]{:S(2)}) %collective-permute-start.3) | collective-permute-done | bytes 131104 | tf_op jit(solution)/shard_map/ppermute | solution.py:25
  37.1 0.0 copy-done.3
  37.1 1.7 %gather.1 = f32[32,4096]{1,0:T(8,128)} custom-call(s32[1,48]{1,0:T(1,128)S(1)} %copy-done.3, bf16[512,128]{1,0:T(8,128)(2,1)S(1)} %collective-permute-done.2.left, f32[512,128]{1,0:T(8,128)S(1)} %get-tuple-element.19.mid, bf16[512,128]{1,0:T(8,128)(2,1)S(1)} %collective-permute-done.3.right), custom_call_target="tpu_custom_call" | custom-call | tf_op jit(solution)/shard_map/gather/pallas_call | solution.py:256
Async XLA Ops:
  0.0 14.0 %collective-permute-start.1 = (bf16[16,64,64]{2,1,0:T(8,128)(2,1)}, bf16[16,64,64]{2,1,0:T(8,128)(2,1)S(1)}, u32[]{:S(2)}, u32[]{:S(2)}) collective-permute-start(bf16[16,64,64]{2,1,0:T(8,128)(2,1)} %own.1), channel_id=1, source_target_pairs={{0,63},{1,0},{2,1},{3,2},{4,3},{5,4},{6,5},{7,6},{8,7},{9,8},{10,9... | collective-permute-start | bytes 393224 | tf_op jit(solution)/shard_map/ppermute | solution.py:25
  5.1 10.0 %collective-permute-start = (bf16[16,64,64]{2,1,0:T(8,128)(2,1)}, bf16[16,64,64]{2,1,0:T(8,128)(2,1)S(1)}, u32[]{:S(2)}, u32[]{:S(2)}) collective-permute-start(bf16[16,64,64]{2,1,0:T(8,128)(2,1)} %own.1), channel_id=1, source_target_pairs={{0,1},{1,2},{2,3},{3,4},{4,5},{5,6},{6,7},{7,8},{8,9},{9,10},{10,1... | collective-permute-start | bytes 393224 | tf_op jit(solution)/shard_map/ppermute | solution.py:25
  7.0 1.0 %copy-start = (bf16[16,64,64]{2,1,0:T(8,128)(2,1)S(1)}, bf16[16,64,64]{2,1,0:T(8,128)(2,1)}, u32[]{:S(2)}) copy-start(bf16[16,64,64]{2,1,0:T(8,128)(2,1)} %own.1) | copy-start | bytes 393220
  8.0 0.7 %copy-start.1 = (s32[16,27]{1,0:T(8,128)S(1)}, s32[16,27]{1,0:T(8,128)}, u32[]{:S(2)}) copy-start(s32[16,27]{1,0:T(8,128)} %cols.1) | copy-start | bytes 5188
  8.7 0.7 %copy-start.2 = (s32[16,27]{1,0:T(8,128)S(1)}, s32[16,27]{1,0:T(8,128)}, u32[]{:S(2)}) copy-start(s32[16,27]{1,0:T(8,128)} %slots.1) | copy-start | bytes 5188
  9.4 27.7 %copy-start.3 = (s32[1,48]{1,0:T(1,128)S(1)}, s32[1,48]{1,0:T(1,128)}, u32[]{:S(2)}) copy-start(s32[1,48]{1,0:T(1,128)} %into.1) | copy-start | bytes 580
  18.0 17.5 %collective-permute-start.2 = (bf16[512,128]{1,0:T(8,128)(2,1)S(1)}, bf16[512,128]{1,0:T(8,128)(2,1)S(1)}, u32[]{:S(2)}, u32[]{:S(2)}) collective-permute-start(bf16[512,128]{1,0:T(8,128)(2,1)S(1)} %get-tuple-element.18), channel_id=1, source_target_pairs={{0,64},{64,128},{128,192},{192,256},{256,320},{320,384},{384,448},... | collective-permute-start | bytes 393224 | tf_op jit(solution)/shard_map/ppermute | solution.py:25
  22.3 14.7 %collective-permute-start.3 = (bf16[512,128]{1,0:T(8,128)(2,1)S(1)}, bf16[512,128]{1,0:T(8,128)(2,1)S(1)}, u32[]{:S(2)}, u32[]{:S(2)}) collective-permute-start(bf16[512,128]{1,0:T(8,128)(2,1)S(1)} %get-tuple-element.20), channel_id=1, source_target_pairs={{0,704},{64,0},{128,64},{192,128},{256,192},{320,256},{384,320},{4... | collective-permute-start | bytes 393224 | tf_op jit(solution)/shard_map/ppermute | solution.py:25

commit v3 on v2

--- a/solution.py
+++ b/solution.py
@@ -233,7 +233,7 @@
         compiler_params=pltpu.CompilerParams(vmem_limit_bytes=46 << 20),
         cost_estimate=pl.CostEstimate(flops=10**9, bytes_accessed=12 * 10**6, transcendentals=0),
         name="near",
-    )(matrix_blocks, prolong, columns, partial_slot)
+    )(*(pltpu.with_memory_space_constraint(v, pltpu.HBM) for v in (matrix_blocks, prolong, columns, partial_slot)))
     up, mid, down = pl.pallas_call(
         far_kernel,
         out_shape=(sent, jax.ShapeDtypeStruct(third, F32), sent),

time: 39 us -> 39.1 us (level)
  local copies, waits for them, and re-layouts: 2.34 us -> 0.01 us
  Pallas kernels: 9.23 us -> 11.1 us
  waiting for transfers between devices: 3.58 us -> 4.07 us
    unnamed x8 -> x2, local copies, waits for them, and re-layouts: 2.34 us -> 0.01 us
    pallas_call x1, Pallas kernels: 4.64 us -> 6.5 us  [per_device(): pl.pallas_call(near_kernel, out_shape=(jax.ShapeDtypeStruct((DEPTH, 9 * W...]
    ppermute x4, waiting for transfers between devices: 3.58 us -> 4.07 us  [shifted(): return lax.ppermute(value, axis, pairs)]
  transfers between devices with their start and end apart: 4 -> 4, of which waited for: 3 -> 3; matrix products, arithmetic and copies ran while one was open for 0% -> 0% of each run, Pallas kernels for 12% -> 17%
where the time goes in v3:
time: 39.1 us; the launch traced here: 38.8 us
  starting transfers between devices  23.6 us (60%)
  Pallas kernels  11.1 us (28%)
  waiting for transfers between devices  4.07 us (10%)
    ppermute x4, starting transfers between devices, shifted(): return lax.ppermute(value, axis, pairs)  23.6 us
    pallas_call x1, Pallas kernels, per_device(): pl.pallas_call(near_kernel, out_shape=(jax.ShapeDtypeStruct((DEPTH, 9 * W...  6.5 us
    ppermute x4, waiting for transfers between devices, shifted(): return lax.ppermute(value, axis, pairs)  4.07 us
    pallas_call x1, Pallas kernels, per_device(): pl.pallas_call(far_kernel, out_shape=(sent, jax.ShapeDtypeStruct(third, F...  2.93 us
    pallas_call x1, Pallas kernels, per_device(): pl.pallas_call(gather_kernel, out_shape=jax.ShapeDtypeStruct((SLOTS, W *...  1.66 us
  transfers between devices with their start and end apart: 4, of which 3 were waited for; matrix products, arithmetic and copies ran while one was open for 0% of the time, Pallas kernels for 17%

profile of v3, /device:TPU:6, one launch (start us, length us, event | category | flops | bytes accessed | tf_op | source)
XLA Modules:
  0.0 38.8 jit_solution(3441174095590243790)
XLA Ops:
  0.0 0.0 copy-start
  0.0 5.2 %collective-permute-start.1 = (bf16[16,64,64]{2,1,0:T(8,128)(2,1)}, bf16[16,64,64]{2,1,0:T(8,128)(2,1)S(1)}, u32[]{:S(2)}, u32[]{:S(2)}) collective-permute-start(bf16[16,64,64]{2,1,0:T(8,128)(2,1)} %own.1), channel_id=1, source_target_pairs={{0,63},{1,0},{2,1},{3,2},{4,3},{5,4},{6,5},{7,6},{8,7},{9,8},{10,9... | collective-permute-start | bytes 393224 | tf_op jit(solution)/shard_map/ppermute | solution.py:25
  5.2 1.9 %collective-permute-start = (bf16[16,64,64]{2,1,0:T(8,128)(2,1)}, bf16[16,64,64]{2,1,0:T(8,128)(2,1)S(1)}, u32[]{:S(2)}, u32[]{:S(2)}) collective-permute-start(bf16[16,64,64]{2,1,0:T(8,128)(2,1)} %own.1), channel_id=1, source_target_pairs={{0,1},{1,2},{2,3},{3,4},{4,5},{5,6},{6,7},{7,8},{8,9},{9,10},{10,1... | collective-permute-start | bytes 393224 | tf_op jit(solution)/shard_map/ppermute | solution.py:25
  7.1 6.5 %near.1 = (bf16[8,576,256]{2,1,0:T(8,128)(2,1)S(1)}, f32[1536,128]{1,0:T(8,128)S(1)}, f32[1536,128]{1,0:T(8,128)S(1)}, s32[16,27]{1,0:T(8,128)S(1)}, bf16[16,64,64]{2,1,0:T(8,128)(2,1)S(1)}) custom-call(bf16[16,27,64,64]{3,2,1,0:T(8,128)(2,1)} %blocks.1, bf16[16,64,64]{2,1,0:T(8,128)(2,1)} %own.1, s32[16,27]{1,0:T(8,128)} %cols.1, s32[16,27]{1,0:T(8,128)} %slots.1), custom_call_target="tpu_custom_call" | custom-call | flops 1000000000 | bytes 12000000 | tf_op jit(solution)/shard_map/near/pallas_call | solution.py:211
  13.6 0.0 collective-permute-done.1.after
  13.7 1.6 %collective-permute-done.before = bf16[16,64,64]{2,1,0:T(8,128)(2,1)S(1)} collective-permute-done((bf16[16,64,64]{2,1,0:T(8,128)(2,1)}, bf16[16,64,64]{2,1,0:T(8,128)(2,1)S(1)}, u32[]{:S(2)}, u32[]{:S(2)}) %collective-permute-start) | collective-permute-done | bytes 131104 | tf_op jit(solution)/shard_map/ppermute | solution.py:25
  15.2 2.9 %far.1 = (bf16[512,128]{1,0:T(8,128)(2,1)S(1)}, f32[512,128]{1,0:T(8,128)S(1)}, bf16[512,128]{1,0:T(8,128)(2,1)S(1)}) custom-call(s32[16,27]{1,0:T(8,128)S(1)} %get-tuple-element.13.table, bf16[8,576,256]{2,1,0:T(8,128)(2,1)S(1)} %get-tuple-element.14.blocks, f32[1536,128]{1,0:T(8,128)S(1)} %get-tuple-element.15.near_a, ...), custom_call_target="tpu_custom_call" | custom-call | tf_op jit(solution)/shard_map/far/pallas_call | solution.py:237
  18.2 4.3 %collective-permute-start.2 = (bf16[512,128]{1,0:T(8,128)(2,1)S(1)}, bf16[512,128]{1,0:T(8,128)(2,1)S(1)}, u32[]{:S(2)}, u32[]{:S(2)}) collective-permute-start(bf16[512,128]{1,0:T(8,128)(2,1)S(1)} %get-tuple-element.18), channel_id=1, source_target_pairs={{0,64},{64,128},{128,192},{192,256},{256,320},{320,384},{384,448},... | collective-permute-start | bytes 393224 | tf_op jit(solution)/shard_map/ppermute | solution.py:25
  22.4 12.2 %collective-permute-start.3 = (bf16[512,128]{1,0:T(8,128)(2,1)S(1)}, bf16[512,128]{1,0:T(8,128)(2,1)S(1)}, u32[]{:S(2)}, u32[]{:S(2)}) collective-permute-start(bf16[512,128]{1,0:T(8,128)(2,1)S(1)} %get-tuple-element.20), channel_id=1, source_target_pairs={{0,704},{64,0},{128,64},{192,128},{256,192},{320,256},{384,320},{4... | collective-permute-start | bytes 393224 | tf_op jit(solution)/shard_map/ppermute | solution.py:25
  34.7 1.0 %collective-permute-done.2.left = bf16[512,128]{1,0:T(8,128)(2,1)S(1)} collective-permute-done((bf16[512,128]{1,0:T(8,128)(2,1)S(1)}, bf16[512,128]{1,0:T(8,128)(2,1)S(1)}, u32[]{:S(2)}, u32[]{:S(2)}) %collective-permute-start.2) | collective-permute-done | bytes 131104 | tf_op jit(solution)/shard_map/ppermute | solution.py:25
  35.7 1.5 %collective-permute-done.3.right = bf16[512,128]{1,0:T(8,128)(2,1)S(1)} collective-permute-done((bf16[512,128]{1,0:T(8,128)(2,1)S(1)}, bf16[512,128]{1,0:T(8,128)(2,1)S(1)}, u32[]{:S(2)}, u32[]{:S(2)}) %collective-permute-start.3) | collective-permute-done | bytes 131104 | tf_op jit(solution)/shard_map/ppermute | solution.py:25
  37.2 0.0 copy-done
  37.2 1.7 %gather.1 = f32[32,4096]{1,0:T(8,128)} custom-call(s32[1,48]{1,0:T(1,128)S(1)} %copy-done, bf16[512,128]{1,0:T(8,128)(2,1)S(1)} %collective-permute-done.2.left, f32[512,128]{1,0:T(8,128)S(1)} %get-tuple-element.19.mid, bf16[512,128]{1,0:T(8,128)(2,1)S(1)} %collective-permute-done.3.right), custom_call_target="tpu_custom_call" | custom-call | tf_op jit(solution)/shard_map/gather/pallas_call | solution.py:256
Async XLA Ops:
  0.0 37.2 %copy-start = (s32[1,48]{1,0:T(1,128)S(1)}, s32[1,48]{1,0:T(1,128)}, u32[]{:S(2)}) copy-start(s32[1,48]{1,0:T(1,128)} %into.1) | copy-start | bytes 580
  0.0 13.6 %collective-permute-start.1 = (bf16[16,64,64]{2,1,0:T(8,128)(2,1)}, bf16[16,64,64]{2,1,0:T(8,128)(2,1)S(1)}, u32[]{:S(2)}, u32[]{:S(2)}) collective-permute-start(bf16[16,64,64]{2,1,0:T(8,128)(2,1)} %own.1), channel_id=1, source_target_pairs={{0,63},{1,0},{2,1},{3,2},{4,3},{5,4},{6,5},{7,6},{8,7},{9,8},{10,9... | collective-permute-start | bytes 393224 | tf_op jit(solution)/shard_map/ppermute | solution.py:25
  5.2 10.0 %collective-permute-start = (bf16[16,64,64]{2,1,0:T(8,128)(2,1)}, bf16[16,64,64]{2,1,0:T(8,128)(2,1)S(1)}, u32[]{:S(2)}, u32[]{:S(2)}) collective-permute-start(bf16[16,64,64]{2,1,0:T(8,128)(2,1)} %own.1), channel_id=1, source_target_pairs={{0,1},{1,2},{2,3},{3,4},{4,5},{5,6},{6,7},{7,8},{8,9},{9,10},{10,1... | collective-permute-start | bytes 393224 | tf_op jit(solution)/shard_map/ppermute | solution.py:25
  18.2 17.5 %collective-permute-start.2 = (bf16[512,128]{1,0:T(8,128)(2,1)S(1)}, bf16[512,128]{1,0:T(8,128)(2,1)S(1)}, u32[]{:S(2)}, u32[]{:S(2)}) collective-permute-start(bf16[512,128]{1,0:T(8,128)(2,1)S(1)} %get-tuple-element.18), channel_id=1, source_target_pairs={{0,64},{64,128},{128,192},{192,256},{256,320},{320,384},{384,448},... | collective-permute-start | bytes 393224 | tf_op jit(solution)/shard_map/ppermute | solution.py:25
  22.4 14.7 %collective-permute-start.3 = (bf16[512,128]{1,0:T(8,128)(2,1)S(1)}, bf16[512,128]{1,0:T(8,128)(2,1)S(1)}, u32[]{:S(2)}, u32[]{:S(2)}) collective-permute-start(bf16[512,128]{1,0:T(8,128)(2,1)S(1)} %get-tuple-element.20), channel_id=1, source_target_pairs={{0,704},{64,0},{128,64},{192,128},{256,192},{320,256},{384,320},{4... | collective-permute-start | bytes 393224 | tf_op jit(solution)/shard_map/ppermute | solution.py:25

commit v4 on v3

--- a/solution.py
+++ b/solution.py
@@ -16,7 +16,14 @@
 LAYERS = 64
 F32 = jnp.float32
 BF = jnp.bfloat16
-UNROLL_NEAR, UNROLL_FAR, UNROLL_STRIP = 8, 4, 8
+UNROLL_FAR, UNROLL_STRIP = 8, 8
+STEPS = (
+    ((7, 0, 1), (0,), ()),
+    ((2, 3), (1, 2), ()),
+    ((4, 5), (3, 4), (1,)),
+    ((6,), (5, 6, 7), (2, 3)),
+    ((), (), (0, 4, 5, 6, 7)),
+)
 
 
 def shifted(value, axis, steps):
@@ -109,8 +116,6 @@
         return held[i, look[i, d * 9 + u * 3 + g] >> 6]
 
     def repack(z):
-        for copy in fetches(z):
-            copy.wait()
         for x in range(2):
             for u in range(3):
                 for g in range(3):
@@ -120,11 +125,7 @@
                     pair = jnp.concatenate([block(i, 0, u, g), block(i, 2, u, g)], axis=1)
                     far[(z + g - 1) & (DEPTH - 1), at : at + W, side : side + LANES] = pair
 
-    repack(7)
-    repack(0)
-    for z in range(DEPTH):
-        if z < DEPTH - 2:
-            repack(z + 1)
+    def local(z):
         for x in range(2):
             users = [(user(x, u, g, z), u, g) for u in range(3) for g in range(3)]
             stack = jnp.concatenate([block(i, 1, u, g) for i, u, g in users], axis=0)
@@ -133,15 +134,24 @@
                 lane = W * (e % 2)
                 strip[i, :, W * e : W * e + W] = applied[W * e : W * e + W, lane : lane + W]
 
-    def finish(i, carry):
-        add_strip(left[i], strip[i], (acc_a, acc_b), lambda e: look[i, 9 + e] & (W - 1), 9)
-        return carry
-
-    lax.fori_loop(0, ROWS, finish, 0, unroll=UNROLL_NEAR)
+    def finish(z):
+        for i in (z, z + DEPTH):
+            add_strip(left[i], strip[i], (acc_a, acc_b), lambda e: look[i, 9 + e] & (W - 1), 9)
+
+    for arrived, complete, ready in STEPS:
+        for z in arrived:
+            for copy in fetches(z):
+                copy.wait()
+        for z in ready:
+            finish(z)
+        for z in arrived:
+            repack(z)
+        for z in complete:
+            local(z)
 
 
 def far_kernel(
-    table, blocks, near_a, near_b, left, before, after, up, mid, down,
+    table, blocks, near_a, near_b, left, after, before, up, mid, down,
     acc_a, acc_b, look, lows, highs, strip, sems,
 ):
     to_look = pltpu.make_async_copy(table, look, sems.at[0])
@@ -196,72 +206,85 @@
     out[...] = acc[...].reshape(out.shape)
 
 
-def per_device(matrix_blocks, prolong, columns, partial_slot, into_slot):
-    before = shifted(prolong, "inner", 1)
-    after = shifted(prolong, "inner", -1)
-    hbm = pl.BlockSpec(memory_space=pltpu.HBM)
-    vmem = pl.BlockSpec(memory_space=pltpu.VMEM)
-    smem = pl.BlockSpec(memory_space=pltpu.SMEM)
-    sums = jax.ShapeDtypeStruct((3 * BUF * HALF, LANES), F32)
-    third = (BUF * HALF, LANES)
-    sent = jax.ShapeDtypeStruct(third, BF)
-    table_v = pltpu.VMEM((ROWS, NBR), jnp.int32)
-    table_s = pltpu.SMEM((ROWS, NBR), jnp.int32)
-    wide = pltpu.VMEM((ROWS, W, LANES), BF)
-    far, acc_a, acc_b, table, left = pl.pallas_call(
+HBM = pl.BlockSpec(memory_space=pltpu.HBM)
+VMEM = pl.BlockSpec(memory_space=pltpu.VMEM)
+SMEM = pl.BlockSpec(memory_space=pltpu.SMEM)
+SUMS = jax.ShapeDtypeStruct((3 * BUF * HALF, LANES), F32)
+THIRD = (BUF * HALF, LANES)
+TABLE = (ROWS, NBR)
+WIDE = pltpu.VMEM((ROWS, W, LANES), BF)
+
+
+def near(*operands):
+    return pl.pallas_call(
         near_kernel,
         out_shape=(
             jax.ShapeDtypeStruct((DEPTH, 9 * W, 4 * W), BF),
-            sums,
-            sums,
-            jax.ShapeDtypeStruct((ROWS, NBR), jnp.int32),
+            SUMS,
+            SUMS,
+            jax.ShapeDtypeStruct(TABLE, jnp.int32),
             jax.ShapeDtypeStruct((ROWS, W, W), BF),
         ),
-        in_specs=[hbm] * 4,
-        out_specs=(vmem,) * 5,
+        in_specs=[HBM] * 4,
+        out_specs=(VMEM,) * 5,
         scratch_shapes=[
             pltpu.VMEM((ROWS, NBR, W, W), BF),
             pltpu.VMEM((ROWS, W, W), BF),
-            table_v,
-            table_v,
-            table_s,
-            wide,
+            pltpu.VMEM(TABLE, jnp.int32),
+            pltpu.VMEM(TABLE, jnp.int32),
+            pltpu.SMEM(TABLE, jnp.int32),
+            WIDE,
             pltpu.VMEM((ROWS, W, 10 * W), BF),
             pltpu.SemaphoreType.DMA((4,)),
             pltpu.SemaphoreType.DMA((ROWS,)),
         ],
-        compiler_params=pltpu.CompilerParams(vmem_limit_bytes=46 << 20),
+        compiler_params=pltpu.CompilerParams(vmem_limit_bytes=40 << 20),
         cost_estimate=pl.CostEstimate(flops=10**9, bytes_accessed=12 * 10**6, transcendentals=0),
         name="near",
-    )(*(pltpu.with_memory_space_constraint(v, pltpu.HBM) for v in (matrix_blocks, prolong, columns, partial_slot)))
-    up, mid, down = pl.pallas_call(
+    )(*(pltpu.with_memory_space_constraint(value, pltpu.HBM) for value in operands))
+
+
+def far(*operands):
+    sent = jax.ShapeDtypeStruct(THIRD, BF)
+    return pl.pallas_call(
         far_kernel,
-        out_shape=(sent, jax.ShapeDtypeStruct(third, F32), sent),
-        in_specs=[vmem] * 7,
-        out_specs=(vmem,) * 3,
+        out_shape=(sent, jax.ShapeDtypeStruct(THIRD, F32), sent),
+        in_specs=[VMEM] * 7,
+        out_specs=(VMEM,) * 3,
         scratch_shapes=[
-            pltpu.VMEM(sums.shape, F32),
-            pltpu.VMEM(sums.shape, F32),
-            table_s,
-            wide,
-            wide,
+            pltpu.VMEM(SUMS.shape, F32),
+            pltpu.VMEM(SUMS.shape, F32),
+            pltpu.SMEM(TABLE, jnp.int32),
+            WIDE,
+            WIDE,
             pltpu.VMEM((ROWS, W, 18 * W), BF),
             pltpu.SemaphoreType.DMA((1,)),
         ],
         compiler_params=pltpu.CompilerParams(vmem_limit_bytes=24 << 20),
         name="far",
-    )(table, far, acc_a, acc_b, left, before, after)
-    from_left = shifted(up, "slab", 1)
-    from_right = shifted(down, "slab", -1)
+    )(*operands)
+
+
+def gather(*operands):
     return pl.pallas_call(
         gather_kernel,
         out_shape=jax.ShapeDtypeStruct((SLOTS, W * W), F32),
-        in_specs=[smem, vmem, vmem, vmem],
-        out_specs=vmem,
+        in_specs=[SMEM, VMEM, VMEM, VMEM],
+        out_specs=VMEM,
         scratch_shapes=[pltpu.VMEM((SLOTS * HALF, LANES), F32)],
         compiler_params=pltpu.CompilerParams(vmem_limit_bytes=16 << 20),
         name="gather",
-    )(into_slot, from_left, mid, from_right)
+    )(*operands)
+
+
+def per_device(matrix_blocks, prolong, columns, partial_slot, into_slot):
+    before = shifted(prolong, "inner", 1)
+    after = shifted(prolong, "inner", -1)
+    blocks, acc_a, acc_b, table, left = near(matrix_blocks, prolong, columns, partial_slot)
+    up, mid, down = far(table, blocks, acc_a, acc_b, left, after, before)
+    from_left = shifted(up, "slab", 1)
+    from_right = shifted(down, "slab", -1)
+    return gather(into_slot, from_left, mid, from_right)
 
 
 def solution(mesh):

time: 39.1 us -> 37.3 us (0.954)
  waiting for transfers between devices: 4.07 us -> 2.5 us
  Pallas kernels: 11.1 us -> 10.2 us
  starting transfers between devices: 23.6 us -> 24.3 us
    ppermute x4, waiting for transfers between devices: 4.07 us -> 2.5 us  [shifted(): return lax.ppermute(value, axis, pairs)]
    pallas_call x3, Pallas kernels: 11.1 us -> 10.2 us  [the longest x1 5.8 us: near(): pl.pallas_call(near_kernel, out_shape=(jax.ShapeDtypeStruct((DEPTH, 9 * W...]
    ppermute x4, starting transfers between devices: 23.6 us -> 24.3 us  [shifted(): return lax.ppermute(value, axis, pairs)]
  transfers between devices with their start and end apart: 4 -> 4, of which waited for: 3 -> 2; matrix products, arithmetic and copies ran while one was open for 0% -> 0% of each run, Pallas kernels for 17% -> 16%
where the time goes in v4:
time: 37.3 us; the launch traced here: 37.1 us
  starting transfers between devices  24.3 us (65%)
  Pallas kernels  10.2 us (27%)
  waiting for transfers between devices  2.5 us (7%)
    ppermute x4, starting transfers between devices, shifted(): return lax.ppermute(value, axis, pairs)  24.3 us
    pallas_call x1, Pallas kernels, near(): pl.pallas_call(near_kernel, out_shape=(jax.ShapeDtypeStruct((DEPTH, 9 * W...  5.8 us
    pallas_call x1, Pallas kernels, far(): pl.pallas_call(far_kernel, out_shape=(sent, jax.ShapeDtypeStruct(THIRD, F...  2.76 us
    ppermute x4, waiting for transfers between devices, shifted(): return lax.ppermute(value, axis, pairs)  2.5 us
    pallas_call x1, Pallas kernels, gather(): pl.pallas_call(gather_kernel, out_shape=jax.ShapeDtypeStruct((SLOTS, W *...  1.66 us
  transfers between devices with their start and end apart: 4, of which 2 were waited for; matrix products, arithmetic and copies ran while one was open for 0% of the time, Pallas kernels for 16%

profile of v4, /device:TPU:6, one launch (start us, length us, event | category | flops | bytes accessed | tf_op | source)
XLA Modules:
  0.0 37.1 jit_solution(1132409103869770866)
XLA Ops:
  0.0 0.0 copy-start
  0.0 2.0 %collective-permute-start.1 = (bf16[16,64,64]{2,1,0:T(8,128)(2,1)}, bf16[16,64,64]{2,1,0:T(8,128)(2,1)S(1)}, u32[]{:S(2)}, u32[]{:S(2)}) collective-permute-start(bf16[16,64,64]{2,1,0:T(8,128)(2,1)} %own.1), channel_id=1, source_target_pairs={{0,1},{1,2},{2,3},{3,4},{4,5},{5,6},{6,7},{7,8},{8,9},{9,10},{10,1... | collective-permute-start | bytes 393224 | tf_op jit(solution)/shard_map/ppermute | solution.py:32
  2.0 5.8 %collective-permute-start = (bf16[16,64,64]{2,1,0:T(8,128)(2,1)}, bf16[16,64,64]{2,1,0:T(8,128)(2,1)S(1)}, u32[]{:S(2)}, u32[]{:S(2)}) collective-permute-start(bf16[16,64,64]{2,1,0:T(8,128)(2,1)} %own.1), channel_id=1, source_target_pairs={{0,63},{1,0},{2,1},{3,2},{4,3},{5,4},{6,5},{7,6},{8,7},{9,8},{10,9... | collective-permute-start | bytes 393224 | tf_op jit(solution)/shard_map/ppermute | solution.py:32
  7.8 5.8 %near.1 = (bf16[8,576,256]{2,1,0:T(8,128)(2,1)S(1)}, f32[1536,128]{1,0:T(8,128)S(1)}, f32[1536,128]{1,0:T(8,128)S(1)}, s32[16,27]{1,0:T(8,128)S(1)}, bf16[16,64,64]{2,1,0:T(8,128)(2,1)S(1)}) custom-call(bf16[16,27,64,64]{3,2,1,0:T(8,128)(2,1)} %blocks.1, bf16[16,64,64]{2,1,0:T(8,128)(2,1)} %own.1, s32[16,27]{1,0:T(8,128)} %cols.1, s32[16,27]{1,0:T(8,128)} %slots.1), custom_call_target="tpu_custom_call" | custom-call | flops 1000000000 | bytes 12000000 | tf_op jit(solution)/shard_map/near/pallas_call | solution.py:219
  13.6 0.0 collective-permute-done.1.before
  13.6 0.0 collective-permute-done.after
  13.6 2.8 %far.1 = (bf16[512,128]{1,0:T(8,128)(2,1)S(1)}, f32[512,128]{1,0:T(8,128)S(1)}, bf16[512,128]{1,0:T(8,128)(2,1)S(1)}) custom-call(s32[16,27]{1,0:T(8,128)S(1)} %get-tuple-element.13.table, bf16[8,576,256]{2,1,0:T(8,128)(2,1)S(1)} %get-tuple-element.14.blocks, f32[1536,128]{1,0:T(8,128)S(1)} %get-tuple-element.15.near_a, ...), custom_call_target="tpu_custom_call" | custom-call | tf_op jit(solution)/shard_map/far/pallas_call | solution.py:249
  16.4 4.3 %collective-permute-start.2 = (bf16[512,128]{1,0:T(8,128)(2,1)S(1)}, bf16[512,128]{1,0:T(8,128)(2,1)S(1)}, u32[]{:S(2)}, u32[]{:S(2)}) collective-permute-start(bf16[512,128]{1,0:T(8,128)(2,1)S(1)} %get-tuple-element.18), channel_id=1, source_target_pairs={{0,64},{64,128},{128,192},{192,256},{256,320},{320,384},{384,448},... | collective-permute-start | bytes 393224 | tf_op jit(solution)/shard_map/ppermute | solution.py:32
  20.7 12.2 %collective-permute-start.3 = (bf16[512,128]{1,0:T(8,128)(2,1)S(1)}, bf16[512,128]{1,0:T(8,128)(2,1)S(1)}, u32[]{:S(2)}, u32[]{:S(2)}) collective-permute-start(bf16[512,128]{1,0:T(8,128)(2,1)S(1)} %get-tuple-element.20), channel_id=1, source_target_pairs={{0,704},{64,0},{128,64},{192,128},{256,192},{320,256},{384,320},{4... | collective-permute-start | bytes 393224 | tf_op jit(solution)/shard_map/ppermute | solution.py:32
  32.9 1.0 %collective-permute-done.2.left = bf16[512,128]{1,0:T(8,128)(2,1)S(1)} collective-permute-done((bf16[512,128]{1,0:T(8,128)(2,1)S(1)}, bf16[512,128]{1,0:T(8,128)(2,1)S(1)}, u32[]{:S(2)}, u32[]{:S(2)}) %collective-permute-start.2) | collective-permute-done | bytes 131104 | tf_op jit(solution)/shard_map/ppermute | solution.py:32
  33.9 1.5 %collective-permute-done.3.right = bf16[512,128]{1,0:T(8,128)(2,1)S(1)} collective-permute-done((bf16[512,128]{1,0:T(8,128)(2,1)S(1)}, bf16[512,128]{1,0:T(8,128)(2,1)S(1)}, u32[]{:S(2)}, u32[]{:S(2)}) %collective-permute-start.3) | collective-permute-done | bytes 131104 | tf_op jit(solution)/shard_map/ppermute | solution.py:32
  35.4 0.0 copy-done
  35.4 1.7 %gather.1 = f32[32,4096]{1,0:T(8,128)} custom-call(s32[1,48]{1,0:T(1,128)S(1)} %copy-done, bf16[512,128]{1,0:T(8,128)(2,1)S(1)} %collective-permute-done.2.left, f32[512,128]{1,0:T(8,128)S(1)} %get-tuple-element.19.mid, bf16[512,128]{1,0:T(8,128)(2,1)S(1)} %collective-permute-done.3.right), custom_call_target="tpu_custom_call" | custom-call | tf_op jit(solution)/shard_map/gather/pallas_call | solution.py:269
Async XLA Ops:
  0.0 35.4 %copy-start = (s32[1,48]{1,0:T(1,128)S(1)}, s32[1,48]{1,0:T(1,128)}, u32[]{:S(2)}) copy-start(s32[1,48]{1,0:T(1,128)} %into.1) | copy-start | bytes 580
  0.0 13.6 %collective-permute-start.1 = (bf16[16,64,64]{2,1,0:T(8,128)(2,1)}, bf16[16,64,64]{2,1,0:T(8,128)(2,1)S(1)}, u32[]{:S(2)}, u32[]{:S(2)}) collective-permute-start(bf16[16,64,64]{2,1,0:T(8,128)(2,1)} %own.1), channel_id=1, source_target_pairs={{0,1},{1,2},{2,3},{3,4},{4,5},{5,6},{6,7},{7,8},{8,9},{9,10},{10,1... | collective-permute-start | bytes 393224 | tf_op jit(solution)/shard_map/ppermute | solution.py:32
  2.0 11.6 %collective-permute-start = (bf16[16,64,64]{2,1,0:T(8,128)(2,1)}, bf16[16,64,64]{2,1,0:T(8,128)(2,1)S(1)}, u32[]{:S(2)}, u32[]{:S(2)}) collective-permute-start(bf16[16,64,64]{2,1,0:T(8,128)(2,1)} %own.1), channel_id=1, source_target_pairs={{0,63},{1,0},{2,1},{3,2},{4,3},{5,4},{6,5},{7,6},{8,7},{9,8},{10,9... | collective-permute-start | bytes 393224 | tf_op jit(solution)/shard_map/ppermute | solution.py:32
  16.4 17.5 %collective-permute-start.2 = (bf16[512,128]{1,0:T(8,128)(2,1)S(1)}, bf16[512,128]{1,0:T(8,128)(2,1)S(1)}, u32[]{:S(2)}, u32[]{:S(2)}) collective-permute-start(bf16[512,128]{1,0:T(8,128)(2,1)S(1)} %get-tuple-element.18), channel_id=1, source_target_pairs={{0,64},{64,128},{128,192},{192,256},{256,320},{320,384},{384,448},... | collective-permute-start | bytes 393224 | tf_op jit(solution)/shard_map/ppermute | solution.py:32
  20.7 14.7 %collective-permute-start.3 = (bf16[512,128]{1,0:T(8,128)(2,1)S(1)}, bf16[512,128]{1,0:T(8,128)(2,1)S(1)}, u32[]{:S(2)}, u32[]{:S(2)}) collective-permute-start(bf16[512,128]{1,0:T(8,128)(2,1)S(1)} %get-tuple-element.20), channel_id=1, source_target_pairs={{0,704},{64,0},{128,64},{192,128},{256,192},{320,256},{384,320},{4... | collective-permute-start | bytes 393224 | tf_op jit(solution)/shard_map/ppermute | solution.py:32

commit v5 on v4

--- a/solution.py
+++ b/solution.py
@@ -16,12 +16,16 @@
 LAYERS = 64
 F32 = jnp.float32
 BF = jnp.bfloat16
-UNROLL_FAR, UNROLL_STRIP = 8, 8
+UNROLL_FAR, UNROLL_STRIP = 8, 16
+AHEAD = 4
 STEPS = (
-    ((7, 0, 1), (0,), ()),
-    ((2, 3), (1, 2), ()),
-    ((4, 5), (3, 4), (1,)),
-    ((6,), (5, 6, 7), (2, 3)),
+    ((7, 0), (), ()),
+    ((1,), (0,), ()),
+    ((2,), (1,), ()),
+    ((3,), (2,), ()),
+    ((4,), (3,), (1,)),
+    ((5,), (4,), (2,)),
+    ((6,), (5, 6, 7), (3,)),
     ((), (), (0, 4, 5, 6, 7)),
 )
 
@@ -90,9 +94,13 @@
             pltpu.make_async_copy(blocks.at[i], held.at[i], row_sems.at[i]) for i in (z, z + DEPTH)
         ]
 
-    for z in (7, 0, 1, 2, 3, 4, 5, 6):
-        for copy in fetches(z):
-            copy.start()
+    def request(step):
+        for z in STEPS[step][0]:
+            for copy in fetches(z):
+                copy.start()
+
+    for step in range(AHEAD):
+        request(step)
     acc_a[...] = jnp.zeros_like(acc_a)
     acc_b[...] = jnp.zeros_like(acc_b)
     small[0].wait()
@@ -138,10 +146,12 @@
         for i in (z, z + DEPTH):
             add_strip(left[i], strip[i], (acc_a, acc_b), lambda e: look[i, 9 + e] & (W - 1), 9)
 
-    for arrived, complete, ready in STEPS:
+    for step, (arrived, complete, ready) in enumerate(STEPS):
         for z in arrived:
             for copy in fetches(z):
                 copy.wait()
+        if step + AHEAD < len(STEPS):
+            request(step + AHEAD)
         for z in ready:
             finish(z)
         for z in arrived:
@@ -198,12 +208,46 @@
         out[...] = (acc_a[rows, :] + acc_b[rows, :]).astype(out.dtype)
 
 
-def gather_kernel(into, left, mid, right, out, acc):
-    acc[...] = jnp.zeros_like(acc)
-    for n, source in enumerate((left, mid, right)):
-        for m in range(BUF):
-            add_to(acc, into[0, n * BUF + m], source[HALF * m : HALF * m + HALF, :].astype(F32))
-    out[...] = acc[...].reshape(out.shape)
+def by_tile(source, blocks):
+    groups = [
+        jnp.concatenate([source[HALF * m + 8 * n : HALF * m + 8 * n + 8, :] for m in range(blocks)], axis=0)
+        for n in range(HALF // 8)
+    ]
+    return jnp.concatenate(groups, axis=1)
+
+
+def route_kernel(into, mid, pick, kept):
+    chosen = jnp.broadcast_to(into[...], (8, 3 * BUF)).astype(F32).astype(BF)
+
+    def one_hot(blocks, source):
+        lanes = 8 * blocks
+        block = lax.broadcasted_iota(jnp.int32, (3 * BUF, lanes), 1) // 8
+        entry = lax.broadcasted_iota(jnp.int32, (3 * BUF, lanes), 0)
+        spread = (entry == source(block)).astype(F32).astype(BF)
+        owner = jnp.dot(chosen, spread, preferred_element_type=F32)[0:1]
+        place = lax.broadcasted_iota(jnp.int32, (SLOTS, lanes), 0).astype(F32)
+        hit = jnp.where(jnp.broadcast_to(owner, (SLOTS, lanes)) == place, 1.0, 0.0)
+        row = lax.broadcasted_iota(jnp.int32, (SLOTS, lanes), 1) & 7
+        return jnp.concatenate([jnp.where(row == t, hit, 0.0) for t in range(8)], axis=0).astype(BF)
+
+    pick[...] = one_hot(2 * BUF, lambda block: jnp.where(block < BUF, block, block + BUF))
+    own = one_hot(BUF, lambda block: block + BUF)
+    value = by_tile(mid, BUF)
+    top = value.astype(BF)
+    rest = value - top.astype(F32)
+    middle = rest.astype(BF)
+    last = (rest - middle.astype(F32)).astype(BF)
+    sums = [jnp.dot(own, part, preferred_element_type=F32) for part in (top, middle, last)]
+    kept[...] = sums[0] + sums[1] + sums[2]
+
+
+def gather_kernel(pick, kept, right, left, out):
+    arrived = jnp.concatenate([by_tile(left, BUF), by_tile(right, BUF)], axis=0)
+    sums = kept[...] + jnp.dot(pick[...], arrived, preferred_element_type=F32)
+    for n in range(HALF // 8):
+        for t in range(8):
+            at = LANES * (8 * n + t)
+            out[:, at : at + LANES] = sums[SLOTS * t : SLOTS * t + SLOTS, LANES * n : LANES * n + LANES]
 
 
 HBM = pl.BlockSpec(memory_space=pltpu.HBM)
@@ -265,13 +309,28 @@
     )(*operands)
 
 
+def route(*operands):
+    rows = 8 * SLOTS
+    return pl.pallas_call(
+        route_kernel,
+        out_shape=(
+            jax.ShapeDtypeStruct((rows, 16 * BUF), BF),
+            jax.ShapeDtypeStruct((rows, LANES * HALF // 8), F32),
+        ),
+        in_specs=[VMEM, VMEM],
+        out_specs=(VMEM, VMEM),
+        compiler_params=pltpu.CompilerParams(vmem_limit_bytes=24 << 20),
+        cost_estimate=pl.CostEstimate(flops=10**9, bytes_accessed=10**7, transcendentals=0),
+        name="route",
+    )(*operands)
+
+
 def gather(*operands):
     return pl.pallas_call(
         gather_kernel,
         out_shape=jax.ShapeDtypeStruct((SLOTS, W * W), F32),
-        in_specs=[SMEM, VMEM, VMEM, VMEM],
+        in_specs=[VMEM] * 4,
         out_specs=VMEM,
-        scratch_shapes=[pltpu.VMEM((SLOTS * HALF, LANES), F32)],
         compiler_params=pltpu.CompilerParams(vmem_limit_bytes=16 << 20),
         name="gather",
     )(*operands)
@@ -284,7 +343,8 @@
     up, mid, down = far(table, blocks, acc_a, acc_b, left, after, before)
     from_left = shifted(up, "slab", 1)
     from_right = shifted(down, "slab", -1)
-    return gather(into_slot, from_left, mid, from_right)
+    pick, kept = route(into_slot, mid)
+    return gather(pick, kept, from_right, from_left)
 
 
 def solution(mesh):

time: 37.3 us -> 40 us (1.072)
  waiting for transfers between devices: 2.5 us -> 5.67 us
  Pallas kernels: 10.2 us -> 9.73 us
    ppermute x4, waiting for transfers between devices: 2.5 us -> 5.67 us  [shifted(): return lax.ppermute(value, axis, pairs)]
    pallas_call x1, Pallas kernels: 1.66 us -> 1.04 us  [gather(): pl.pallas_call(gather_kernel, out_shape=jax.ShapeDtypeStruct((SLOTS, W *...]
    pallas_call x0 -> x1, Pallas kernels: none -> 0.46 us  [route(): pl.pallas_call(route_kernel, out_shape=(jax.ShapeDtypeStruct((rows, 16 *...]
where the time goes in v5:
time: 40 us; the launch traced here: 39.8 us
  starting transfers between devices  24.3 us (61%)
  Pallas kernels  9.73 us (24%)
  waiting for transfers between devices  5.67 us (14%)
    ppermute x4, starting transfers between devices, shifted(): return lax.ppermute(value, axis, pairs)  24.3 us
    pallas_call x1, Pallas kernels, near(): pl.pallas_call(near_kernel, out_shape=(jax.ShapeDtypeStruct((DEPTH, 9 * W...  5.71 us
    ppermute x4, waiting for transfers between devices, shifted(): return lax.ppermute(value, axis, pairs)  5.67 us
    pallas_call x1, Pallas kernels, far(): pl.pallas_call(far_kernel, out_shape=(sent, jax.ShapeDtypeStruct(THIRD, F...  2.52 us
    pallas_call x1, Pallas kernels, gather(): pl.pallas_call(gather_kernel, out_shape=jax.ShapeDtypeStruct((SLOTS, W *...  1.04 us
  transfers between devices with their start and end apart: 4, of which 2 were waited for; matrix products, arithmetic and copies ran while one was open for 0% of the time, Pallas kernels for 16%

profile of v5, /device:TPU:6, one launch (start us, length us, event | category | flops | bytes accessed | tf_op | source)
XLA Modules:
  0.0 39.8 jit_solution(9793209522137449657)
XLA Ops:
  0.0 0.0 copy-start
  0.0 2.0 %collective-permute-start.1 = (bf16[16,64,64]{2,1,0:T(8,128)(2,1)}, bf16[16,64,64]{2,1,0:T(8,128)(2,1)S(1)}, u32[]{:S(2)}, u32[]{:S(2)}) collective-permute-start(bf16[16,64,64]{2,1,0:T(8,128)(2,1)} %own.1), channel_id=1, source_target_pairs={{0,1},{1,2},{2,3},{3,4},{4,5},{5,6},{6,7},{7,8},{8,9},{9,10},{10,1... | collective-permute-start | bytes 393224 | tf_op jit(solution)/shard_map/ppermute | solution.py:36
  2.0 5.8 %collective-permute-start = (bf16[16,64,64]{2,1,0:T(8,128)(2,1)}, bf16[16,64,64]{2,1,0:T(8,128)(2,1)S(1)}, u32[]{:S(2)}, u32[]{:S(2)}) collective-permute-start(bf16[16,64,64]{2,1,0:T(8,128)(2,1)} %own.1), channel_id=1, source_target_pairs={{0,63},{1,0},{2,1},{3,2},{4,3},{5,4},{6,5},{7,6},{8,7},{9,8},{10,9... | collective-permute-start | bytes 393224 | tf_op jit(solution)/shard_map/ppermute | solution.py:36
  7.8 5.7 %near.1 = (bf16[8,576,256]{2,1,0:T(8,128)(2,1)S(1)}, f32[1536,128]{1,0:T(8,128)S(1)}, f32[1536,128]{1,0:T(8,128)S(1)}, s32[16,27]{1,0:T(8,128)S(1)}, bf16[16,64,64]{2,1,0:T(8,128)(2,1)S(1)}) custom-call(bf16[16,27,64,64]{3,2,1,0:T(8,128)(2,1)} %blocks.1, bf16[16,64,64]{2,1,0:T(8,128)(2,1)} %own.1, s32[16,27]{1,0:T(8,128)} %cols.1, s32[16,27]{1,0:T(8,128)} %slots.1), custom_call_target="tpu_custom_call" | custom-call | flops 1000000000 | bytes 12000000 | tf_op jit(solution)/shard_map/near/pallas_call | solution.py:263
  13.5 0.0 collective-permute-done.1.before
  13.5 0.0 collective-permute-done.after
  13.6 2.5 %far.1 = (bf16[512,128]{1,0:T(8,128)(2,1)S(1)}, f32[512,128]{1,0:T(8,128)S(1)}, bf16[512,128]{1,0:T(8,128)(2,1)S(1)}) custom-call(s32[16,27]{1,0:T(8,128)S(1)} %get-tuple-element.15.table, bf16[8,576,256]{2,1,0:T(8,128)(2,1)S(1)} %get-tuple-element.16.blocks, f32[1536,128]{1,0:T(8,128)S(1)} %get-tuple-element.17.near_a, ...), custom_call_target="tpu_custom_call" | custom-call | tf_op jit(solution)/shard_map/far/pallas_call | solution.py:293
  16.1 14.6 %collective-permute-start.2 = (bf16[512,128]{1,0:T(8,128)(2,1)S(1)}, bf16[512,128]{1,0:T(8,128)(2,1)S(1)}, u32[]{:S(2)}, u32[]{:S(2)}) collective-permute-start(bf16[512,128]{1,0:T(8,128)(2,1)S(1)} %get-tuple-element.23), channel_id=1, source_target_pairs={{0,704},{64,0},{128,64},{192,128},{256,192},{320,256},{384,320},{4... | collective-permute-start | bytes 393224 | tf_op jit(solution)/shard_map/ppermute | solution.py:36
  30.7 1.9 %collective-permute-start.3 = (bf16[512,128]{1,0:T(8,128)(2,1)S(1)}, bf16[512,128]{1,0:T(8,128)(2,1)S(1)}, u32[]{:S(2)}, u32[]{:S(2)}) collective-permute-start(bf16[512,128]{1,0:T(8,128)(2,1)S(1)} %get-tuple-element.24), channel_id=1, source_target_pairs={{0,64},{64,128},{128,192},{192,256},{256,320},{320,384},{384,448},... | collective-permute-start | bytes 393224 | tf_op jit(solution)/shard_map/ppermute | solution.py:36
  32.6 0.0 copy-done
  32.6 0.5 %route.1 = (bf16[256,256]{1,0:T(8,128)(2,1)S(1)}, f32[256,512]{1,0:T(8,128)S(1)}) custom-call(s32[1,48]{1,0:T(1,128)S(1)} %copy-done, f32[512,128]{1,0:T(8,128)S(1)} %get-tuple-element.20.mid), custom_call_target="tpu_custom_call" | custom-call | flops 1000000000 | bytes 10000000 | tf_op jit(solution)/shard_map/route/pallas_call | solution.py:314
  33.1 0.1 collective-permute-done.2.right
  33.2 5.6 %collective-permute-done.3.left = bf16[512,128]{1,0:T(8,128)(2,1)S(1)} collective-permute-done((bf16[512,128]{1,0:T(8,128)(2,1)S(1)}, bf16[512,128]{1,0:T(8,128)(2,1)S(1)}, u32[]{:S(2)}, u32[]{:S(2)}) %collective-permute-start.3) | collective-permute-done | bytes 131104 | tf_op jit(solution)/shard_map/ppermute | solution.py:36
  38.7 1.0 %gather.1 = f32[32,4096]{1,0:T(8,128)} custom-call(bf16[256,256]{1,0:T(8,128)(2,1)S(1)} %get-tuple-element.21.pick, f32[256,512]{1,0:T(8,128)S(1)} %get-tuple-element.22.kept, bf16[512,128]{1,0:T(8,128)(2,1)S(1)} %collective-permute-done.2.right, bf16[512,128]{1,0:T(8,128)(2,1)S(1)} %collective-permute-done.3.left), custom_call_target="tpu_custom_call" | custom-call | tf_op jit(solution)/shard_map/gather/pallas_call | solution.py:329
Async XLA Ops:
  0.0 32.6 %copy-start = (s32[1,48]{1,0:T(1,128)S(1)}, s32[1,48]{1,0:T(1,128)}, u32[]{:S(2)}) copy-start(s32[1,48]{1,0:T(1,128)} %into.1) | copy-start | bytes 580
  0.0 13.5 %collective-permute-start.1 = (bf16[16,64,64]{2,1,0:T(8,128)(2,1)}, bf16[16,64,64]{2,1,0:T(8,128)(2,1)S(1)}, u32[]{:S(2)}, u32[]{:S(2)}) collective-permute-start(bf16[16,64,64]{2,1,0:T(8,128)(2,1)} %own.1), channel_id=1, source_target_pairs={{0,1},{1,2},{2,3},{3,4},{4,5},{5,6},{6,7},{7,8},{8,9},{9,10},{10,1... | collective-permute-start | bytes 393224 | tf_op jit(solution)/shard_map/ppermute | solution.py:36
  2.0 11.5 %collective-permute-start = (bf16[16,64,64]{2,1,0:T(8,128)(2,1)}, bf16[16,64,64]{2,1,0:T(8,128)(2,1)S(1)}, u32[]{:S(2)}, u32[]{:S(2)}) collective-permute-start(bf16[16,64,64]{2,1,0:T(8,128)(2,1)} %own.1), channel_id=1, source_target_pairs={{0,63},{1,0},{2,1},{3,2},{4,3},{5,4},{6,5},{7,6},{8,7},{9,8},{10,9... | collective-permute-start | bytes 393224 | tf_op jit(solution)/shard_map/ppermute | solution.py:36
  16.1 17.1 %collective-permute-start.2 = (bf16[512,128]{1,0:T(8,128)(2,1)S(1)}, bf16[512,128]{1,0:T(8,128)(2,1)S(1)}, u32[]{:S(2)}, u32[]{:S(2)}) collective-permute-start(bf16[512,128]{1,0:T(8,128)(2,1)S(1)} %get-tuple-element.23), channel_id=1, source_target_pairs={{0,704},{64,0},{128,64},{192,128},{256,192},{320,256},{384,320},{4... | collective-permute-start | bytes 393224 | tf_op jit(solution)/shard_map/ppermute | solution.py:36
  30.7 8.1 %collective-permute-start.3 = (bf16[512,128]{1,0:T(8,128)(2,1)S(1)}, bf16[512,128]{1,0:T(8,128)(2,1)S(1)}, u32[]{:S(2)}, u32[]{:S(2)}) collective-permute-start(bf16[512,128]{1,0:T(8,128)(2,1)S(1)} %get-tuple-element.24), channel_id=1, source_target_pairs={{0,64},{64,128},{128,192},{192,256},{256,320},{320,384},{384,448},... | collective-permute-start | bytes 393224 | tf_op jit(solution)/shard_map/ppermute | solution.py:36

commit v6 on v5

--- a/solution.py
+++ b/solution.py
@@ -241,7 +241,7 @@
     kept[...] = sums[0] + sums[1] + sums[2]
 
 
-def gather_kernel(pick, kept, right, left, out):
+def gather_kernel(pick, kept, left, right, out):
     arrived = jnp.concatenate([by_tile(left, BUF), by_tile(right, BUF)], axis=0)
     sums = kept[...] + jnp.dot(pick[...], arrived, preferred_element_type=F32)
     for n in range(HALF // 8):
@@ -344,7 +344,7 @@
     from_left = shifted(up, "slab", 1)
     from_right = shifted(down, "slab", -1)
     pick, kept = route(into_slot, mid)
-    return gather(pick, kept, from_right, from_left)
+    return gather(pick, kept, from_left, from_right)
 
 
 def solution(mesh):

time: 40 us -> 36.4 us (0.910)
  waiting for transfers between devices: 5.67 us -> 2.03 us
    ppermute x4, waiting for transfers between devices: 5.67 us -> 2.03 us  [shifted(): return lax.ppermute(value, axis, pairs)]
  transfers between devices with their start and end apart: 4 -> 4, of which waited for: 2 -> 2; matrix products, arithmetic and copies ran while one was open for 0% -> 0% of each run, Pallas kernels for 16% -> 17%
where the time goes in v6:
time: 36.4 us; the launch traced here: 36.1 us
  starting transfers between devices  24.3 us (67%)
  Pallas kernels  9.72 us (27%)
  waiting for transfers between devices  2.03 us (6%)
    ppermute x4, starting transfers between devices, shifted(): return lax.ppermute(value, axis, pairs)  24.3 us
    pallas_call x1, Pallas kernels, near(): pl.pallas_call(near_kernel, out_shape=(jax.ShapeDtypeStruct((DEPTH, 9 * W...  5.71 us
    pallas_call x1, Pallas kernels, far(): pl.pallas_call(far_kernel, out_shape=(sent, jax.ShapeDtypeStruct(THIRD, F...  2.52 us
    ppermute x4, waiting for transfers between devices, shifted(): return lax.ppermute(value, axis, pairs)  2.03 us
    pallas_call x1, Pallas kernels, gather(): pl.pallas_call(gather_kernel, out_shape=jax.ShapeDtypeStruct((SLOTS, W *...  1.04 us
  transfers between devices with their start and end apart: 4, of which 2 were waited for; matrix products, arithmetic and copies ran while one was open for 0% of the time, Pallas kernels for 17%

profile of v6, /device:TPU:6, one launch (start us, length us, event | category | flops | bytes accessed | tf_op | source)
XLA Modules:
  0.0 36.1 jit_solution(11516191423116697959)
XLA Ops:
  0.0 0.0 copy-start
  0.0 2.0 %collective-permute-start.1 = (bf16[16,64,64]{2,1,0:T(8,128)(2,1)}, bf16[16,64,64]{2,1,0:T(8,128)(2,1)S(1)}, u32[]{:S(2)}, u32[]{:S(2)}) collective-permute-start(bf16[16,64,64]{2,1,0:T(8,128)(2,1)} %own.1), channel_id=1, source_target_pairs={{0,1},{1,2},{2,3},{3,4},{4,5},{5,6},{6,7},{7,8},{8,9},{9,10},{10,1... | collective-permute-start | bytes 393224 | tf_op jit(solution)/shard_map/ppermute | solution.py:36
  2.0 5.8 %collective-permute-start = (bf16[16,64,64]{2,1,0:T(8,128)(2,1)}, bf16[16,64,64]{2,1,0:T(8,128)(2,1)S(1)}, u32[]{:S(2)}, u32[]{:S(2)}) collective-permute-start(bf16[16,64,64]{2,1,0:T(8,128)(2,1)} %own.1), channel_id=1, source_target_pairs={{0,63},{1,0},{2,1},{3,2},{4,3},{5,4},{6,5},{7,6},{8,7},{9,8},{10,9... | collective-permute-start | bytes 393224 | tf_op jit(solution)/shard_map/ppermute | solution.py:36
  7.8 5.7 %near.1 = (bf16[8,576,256]{2,1,0:T(8,128)(2,1)S(1)}, f32[1536,128]{1,0:T(8,128)S(1)}, f32[1536,128]{1,0:T(8,128)S(1)}, s32[16,27]{1,0:T(8,128)S(1)}, bf16[16,64,64]{2,1,0:T(8,128)(2,1)S(1)}) custom-call(bf16[16,27,64,64]{3,2,1,0:T(8,128)(2,1)} %blocks.1, bf16[16,64,64]{2,1,0:T(8,128)(2,1)} %own.1, s32[16,27]{1,0:T(8,128)} %cols.1, s32[16,27]{1,0:T(8,128)} %slots.1), custom_call_target="tpu_custom_call" | custom-call | flops 1000000000 | bytes 12000000 | tf_op jit(solution)/shard_map/near/pallas_call | solution.py:263
  13.5 0.0 collective-permute-done.1.before
  13.5 0.0 collective-permute-done.after
  13.6 2.5 %far.1 = (bf16[512,128]{1,0:T(8,128)(2,1)S(1)}, f32[512,128]{1,0:T(8,128)S(1)}, bf16[512,128]{1,0:T(8,128)(2,1)S(1)}) custom-call(s32[16,27]{1,0:T(8,128)S(1)} %get-tuple-element.15.table, bf16[8,576,256]{2,1,0:T(8,128)(2,1)S(1)} %get-tuple-element.16.blocks, f32[1536,128]{1,0:T(8,128)S(1)} %get-tuple-element.17.near_a, ...), custom_call_target="tpu_custom_call" | custom-call | tf_op jit(solution)/shard_map/far/pallas_call | solution.py:293
  16.1 4.3 %collective-permute-start.2 = (bf16[512,128]{1,0:T(8,128)(2,1)S(1)}, bf16[512,128]{1,0:T(8,128)(2,1)S(1)}, u32[]{:S(2)}, u32[]{:S(2)}) collective-permute-start(bf16[512,128]{1,0:T(8,128)(2,1)S(1)} %get-tuple-element.23), channel_id=1, source_target_pairs={{0,64},{64,128},{128,192},{192,256},{256,320},{320,384},{384,448},... | collective-permute-start | bytes 393224 | tf_op jit(solution)/shard_map/ppermute | solution.py:36
  20.3 12.3 %collective-permute-start.3 = (bf16[512,128]{1,0:T(8,128)(2,1)S(1)}, bf16[512,128]{1,0:T(8,128)(2,1)S(1)}, u32[]{:S(2)}, u32[]{:S(2)}) collective-permute-start(bf16[512,128]{1,0:T(8,128)(2,1)S(1)} %get-tuple-element.24), channel_id=1, source_target_pairs={{0,704},{64,0},{128,64},{192,128},{256,192},{320,256},{384,320},{4... | collective-permute-start | bytes 393224 | tf_op jit(solution)/shard_map/ppermute | solution.py:36
  32.6 0.0 copy-done
  32.6 0.5 %route.1 = (bf16[256,256]{1,0:T(8,128)(2,1)S(1)}, f32[256,512]{1,0:T(8,128)S(1)}) custom-call(s32[1,48]{1,0:T(1,128)S(1)} %copy-done, f32[512,128]{1,0:T(8,128)S(1)} %get-tuple-element.20.mid), custom_call_target="tpu_custom_call" | custom-call | flops 1000000000 | bytes 10000000 | tf_op jit(solution)/shard_map/route/pallas_call | solution.py:314
  33.1 0.5 %collective-permute-done.2.left = bf16[512,128]{1,0:T(8,128)(2,1)S(1)} collective-permute-done((bf16[512,128]{1,0:T(8,128)(2,1)S(1)}, bf16[512,128]{1,0:T(8,128)(2,1)S(1)}, u32[]{:S(2)}, u32[]{:S(2)}) %collective-permute-start.2) | collective-permute-done | bytes 131104 | tf_op jit(solution)/shard_map/ppermute | solution.py:36
  33.6 1.5 %collective-permute-done.3.right = bf16[512,128]{1,0:T(8,128)(2,1)S(1)} collective-permute-done((bf16[512,128]{1,0:T(8,128)(2,1)S(1)}, bf16[512,128]{1,0:T(8,128)(2,1)S(1)}, u32[]{:S(2)}, u32[]{:S(2)}) %collective-permute-start.3) | collective-permute-done | bytes 131104 | tf_op jit(solution)/shard_map/ppermute | solution.py:36
  35.1 1.0 %gather.1 = f32[32,4096]{1,0:T(8,128)} custom-call(bf16[256,256]{1,0:T(8,128)(2,1)S(1)} %get-tuple-element.21.pick, f32[256,512]{1,0:T(8,128)S(1)} %get-tuple-element.22.kept, bf16[512,128]{1,0:T(8,128)(2,1)S(1)} %collective-permute-done.2.left, bf16[512,128]{1,0:T(8,128)(2,1)S(1)} %collective-permute-done.3.right), custom_call_target="tpu_custom_call" | custom-call | tf_op jit(solution)/shard_map/gather/pallas_call | solution.py:329
Async XLA Ops:
  0.0 32.6 %copy-start = (s32[1,48]{1,0:T(1,128)S(1)}, s32[1,48]{1,0:T(1,128)}, u32[]{:S(2)}) copy-start(s32[1,48]{1,0:T(1,128)} %into.1) | copy-start | bytes 580
  0.0 13.5 %collective-permute-start.1 = (bf16[16,64,64]{2,1,0:T(8,128)(2,1)}, bf16[16,64,64]{2,1,0:T(8,128)(2,1)S(1)}, u32[]{:S(2)}, u32[]{:S(2)}) collective-permute-start(bf16[16,64,64]{2,1,0:T(8,128)(2,1)} %own.1), channel_id=1, source_target_pairs={{0,1},{1,2},{2,3},{3,4},{4,5},{5,6},{6,7},{7,8},{8,9},{9,10},{10,1... | collective-permute-start | bytes 393224 | tf_op jit(solution)/shard_map/ppermute | solution.py:36
  2.0 11.5 %collective-permute-start = (bf16[16,64,64]{2,1,0:T(8,128)(2,1)}, bf16[16,64,64]{2,1,0:T(8,128)(2,1)S(1)}, u32[]{:S(2)}, u32[]{:S(2)}) collective-permute-start(bf16[16,64,64]{2,1,0:T(8,128)(2,1)} %own.1), channel_id=1, source_target_pairs={{0,63},{1,0},{2,1},{3,2},{4,3},{5,4},{6,5},{7,6},{8,7},{9,8},{10,9... | collective-permute-start | bytes 393224 | tf_op jit(solution)/shard_map/ppermute | solution.py:36
  16.1 17.5 %collective-permute-start.2 = (bf16[512,128]{1,0:T(8,128)(2,1)S(1)}, bf16[512,128]{1,0:T(8,128)(2,1)S(1)}, u32[]{:S(2)}, u32[]{:S(2)}) collective-permute-start(bf16[512,128]{1,0:T(8,128)(2,1)S(1)} %get-tuple-element.23), channel_id=1, source_target_pairs={{0,64},{64,128},{128,192},{192,256},{256,320},{320,384},{384,448},... | collective-permute-start | bytes 393224 | tf_op jit(solution)/shard_map/ppermute | solution.py:36
  20.3 14.8 %collective-permute-start.3 = (bf16[512,128]{1,0:T(8,128)(2,1)S(1)}, bf16[512,128]{1,0:T(8,128)(2,1)S(1)}, u32[]{:S(2)}, u32[]{:S(2)}) collective-permute-start(bf16[512,128]{1,0:T(8,128)(2,1)S(1)} %get-tuple-element.24), channel_id=1, source_target_pairs={{0,704},{64,0},{128,64},{192,128},{256,192},{320,256},{384,320},{4... | collective-permute-start | bytes 393224 | tf_op jit(solution)/shard_map/ppermute | solution.py:36

commit v7 on v6

--- a/solution.py
+++ b/solution.py
@@ -17,7 +17,7 @@
 F32 = jnp.float32
 BF = jnp.bfloat16
 UNROLL_FAR, UNROLL_STRIP = 8, 16
-AHEAD = 4
+FIRST, SECOND = 2, 5
 STEPS = (
     ((7, 0), (), ()),
     ((1,), (0,), ()),
@@ -72,10 +72,10 @@
     low = lax.broadcasted_iota(jnp.int32, (HALF, LANES), 1) < W
     for e in range(0, count, 2):
         even = both[:HALF, W * e : W * e + LANES]
-        odd = both[HALF:, W * e : W * e + LANES]
-        add_to(accs[0], slot_of(e), jnp.where(low, even, pltpu.roll(odd, W, 1)))
+        turned = pltpu.roll(both[HALF:, W * e : W * e + LANES], W, 1)
+        add_to(accs[0], slot_of(e), jnp.where(low, even, turned))
         if e + 1 < count:
-            add_to(accs[1], slot_of(e + 1), jnp.where(low, pltpu.roll(even, W, 1), odd))
+            add_to(accs[1], slot_of(e + 1), jnp.where(low, turned, even))
 
 
 def near_kernel(
@@ -99,12 +99,14 @@
             for copy in fetches(z):
                 copy.start()
 
-    for step in range(AHEAD):
+    for step in range(FIRST):
         request(step)
     acc_a[...] = jnp.zeros_like(acc_a)
     acc_b[...] = jnp.zeros_like(acc_b)
     small[0].wait()
     small[1].wait()
+    for step in range(FIRST, SECOND):
+        request(step)
     table[...] = ordered(cols_v[...], slots_v[...])
     to_look = pltpu.make_async_copy(table, look, sems.at[3])
     to_look.start()
@@ -118,6 +120,8 @@
         left[i] = lax.dot_general(
             split, p, (((1,), (1,)), ((), ())), preferred_element_type=F32
         ).astype(BF)
+    for step in range(SECOND, len(STEPS)):
+        request(step)
     to_look.wait()
 
     def block(i, d, u, g):
@@ -150,8 +154,6 @@
         for z in arrived:
             for copy in fetches(z):
                 copy.wait()
-        if step + AHEAD < len(STEPS):
-            request(step + AHEAD)
         for z in ready:
             finish(z)
         for z in arrived:
@@ -205,7 +207,7 @@
     lax.fori_loop(0, ROWS, finish, 0, unroll=UNROLL_STRIP)
     for n, out in enumerate((down, mid, up)):
         rows = slice(n * BUF * HALF, (n + 1) * BUF * HALF)
-        out[...] = (acc_a[rows, :] + acc_b[rows, :]).astype(out.dtype)
+        out[...] = (acc_a[rows, :] + pltpu.roll(acc_b[rows, :], W, 1)).astype(out.dtype)
 
 
 def by_tile(source, blocks):

time: 36.4 us -> 36.1 us (level)
  the two profiles are of different devices: /device:TPU:6 before, /device:TPU:25 now
where the time goes in v7:
time: 36.1 us; the launch traced here: 35.9 us
  starting transfers between devices  23.2 us (64%)
  Pallas kernels  8.76 us (24%)
  waiting for transfers between devices  3.81 us (11%)
    ppermute x4, starting transfers between devices, shifted(): return lax.ppermute(value, axis, pairs)  23.2 us
    pallas_call x1, Pallas kernels, near(): pl.pallas_call(near_kernel, out_shape=(jax.ShapeDtypeStruct((DEPTH, 9 * W...  4.8 us
    ppermute x4, waiting for transfers between devices, shifted(): return lax.ppermute(value, axis, pairs)  3.81 us
    pallas_call x1, Pallas kernels, far(): pl.pallas_call(far_kernel, out_shape=(sent, jax.ShapeDtypeStruct(THIRD, F...  2.46 us
    pallas_call x1, Pallas kernels, gather(): pl.pallas_call(gather_kernel, out_shape=jax.ShapeDtypeStruct((SLOTS, W *...  1.03 us
  transfers between devices with their start and end apart: 4, of which 2 were waited for; matrix products, arithmetic and copies ran while one was open for 0% of the time, Pallas kernels for 15%

profile of v7, /device:TPU:25, one launch (start us, length us, event | category | flops | bytes accessed | tf_op | source)
XLA Modules:
  0.0 35.9 jit_solution(3712634896778777507)
XLA Ops:
  0.0 0.0 copy-start
  0.0 5.1 %collective-permute-start.1 = (bf16[16,64,64]{2,1,0:T(8,128)(2,1)}, bf16[16,64,64]{2,1,0:T(8,128)(2,1)S(1)}, u32[]{:S(2)}, u32[]{:S(2)}) collective-permute-start(bf16[16,64,64]{2,1,0:T(8,128)(2,1)} %own.1), channel_id=1, source_target_pairs={{0,1},{1,2},{2,3},{3,4},{4,5},{5,6},{6,7},{7,8},{8,9},{9,10},{10,1... | collective-permute-start | bytes 393224 | tf_op jit(solution)/shard_map/ppermute | solution.py:36
  5.1 1.9 %collective-permute-start = (bf16[16,64,64]{2,1,0:T(8,128)(2,1)}, bf16[16,64,64]{2,1,0:T(8,128)(2,1)S(1)}, u32[]{:S(2)}, u32[]{:S(2)}) collective-permute-start(bf16[16,64,64]{2,1,0:T(8,128)(2,1)} %own.1), channel_id=1, source_target_pairs={{0,63},{1,0},{2,1},{3,2},{4,3},{5,4},{6,5},{7,6},{8,7},{9,8},{10,9... | collective-permute-start | bytes 393224 | tf_op jit(solution)/shard_map/ppermute | solution.py:36
  7.0 4.8 %near.1 = (bf16[8,576,256]{2,1,0:T(8,128)(2,1)S(1)}, f32[1536,128]{1,0:T(8,128)S(1)}, f32[1536,128]{1,0:T(8,128)S(1)}, s32[16,27]{1,0:T(8,128)S(1)}, bf16[16,64,64]{2,1,0:T(8,128)(2,1)S(1)}) custom-call(bf16[16,27,64,64]{3,2,1,0:T(8,128)(2,1)} %blocks.1, bf16[16,64,64]{2,1,0:T(8,128)(2,1)} %own.1, s32[16,27]{1,0:T(8,128)} %cols.1, s32[16,27]{1,0:T(8,128)} %slots.1), custom_call_target="tpu_custom_call" | custom-call | flops 1000000000 | bytes 12000000 | tf_op jit(solution)/shard_map/near/pallas_call | solution.py:265
  11.8 0.0 collective-permute-done.1.before
  11.9 2.4 %collective-permute-done.after = bf16[16,64,64]{2,1,0:T(8,128)(2,1)S(1)} collective-permute-done((bf16[16,64,64]{2,1,0:T(8,128)(2,1)}, bf16[16,64,64]{2,1,0:T(8,128)(2,1)S(1)}, u32[]{:S(2)}, u32[]{:S(2)}) %collective-permute-start) | collective-permute-done | bytes 131104 | tf_op jit(solution)/shard_map/ppermute | solution.py:36
  14.2 2.5 %far.1 = (bf16[512,128]{1,0:T(8,128)(2,1)S(1)}, f32[512,128]{1,0:T(8,128)S(1)}, bf16[512,128]{1,0:T(8,128)(2,1)S(1)}) custom-call(s32[16,27]{1,0:T(8,128)S(1)} %get-tuple-element.15.table, bf16[8,576,256]{2,1,0:T(8,128)(2,1)S(1)} %get-tuple-element.16.blocks, f32[1536,128]{1,0:T(8,128)S(1)} %get-tuple-element.17.near_a, ...), custom_call_target="tpu_custom_call" | custom-call | tf_op jit(solution)/shard_map/far/pallas_call | solution.py:295
  16.7 4.0 %collective-permute-start.2 = (bf16[512,128]{1,0:T(8,128)(2,1)S(1)}, bf16[512,128]{1,0:T(8,128)(2,1)S(1)}, u32[]{:S(2)}, u32[]{:S(2)}) collective-permute-start(bf16[512,128]{1,0:T(8,128)(2,1)S(1)} %get-tuple-element.23), channel_id=1, source_target_pairs={{0,64},{64,128},{128,192},{192,256},{256,320},{320,384},{384,448},... | collective-permute-start | bytes 393224 | tf_op jit(solution)/shard_map/ppermute | solution.py:36
  20.7 12.2 %collective-permute-start.3 = (bf16[512,128]{1,0:T(8,128)(2,1)S(1)}, bf16[512,128]{1,0:T(8,128)(2,1)S(1)}, u32[]{:S(2)}, u32[]{:S(2)}) collective-permute-start(bf16[512,128]{1,0:T(8,128)(2,1)S(1)} %get-tuple-element.24), channel_id=1, source_target_pairs={{0,704},{64,0},{128,64},{192,128},{256,192},{320,256},{384,320},{4... | collective-permute-start | bytes 393224 | tf_op jit(solution)/shard_map/ppermute | solution.py:36
  32.9 0.0 copy-done
  32.9 0.5 %route.1 = (bf16[256,256]{1,0:T(8,128)(2,1)S(1)}, f32[256,512]{1,0:T(8,128)S(1)}) custom-call(s32[1,48]{1,0:T(1,128)S(1)} %copy-done, f32[512,128]{1,0:T(8,128)S(1)} %get-tuple-element.20.mid), custom_call_target="tpu_custom_call" | custom-call | flops 1000000000 | bytes 10000000 | tf_op jit(solution)/shard_map/route/pallas_call | solution.py:316
  33.4 0.0 collective-permute-done.2.left
  33.4 1.4 %collective-permute-done.3.right = bf16[512,128]{1,0:T(8,128)(2,1)S(1)} collective-permute-done((bf16[512,128]{1,0:T(8,128)(2,1)S(1)}, bf16[512,128]{1,0:T(8,128)(2,1)S(1)}, u32[]{:S(2)}, u32[]{:S(2)}) %collective-permute-start.3) | collective-permute-done | bytes 131104 | tf_op jit(solution)/shard_map/ppermute | solution.py:36
  34.9 1.0 %gather.1 = f32[32,4096]{1,0:T(8,128)} custom-call(bf16[256,256]{1,0:T(8,128)(2,1)S(1)} %get-tuple-element.21.pick, f32[256,512]{1,0:T(8,128)S(1)} %get-tuple-element.22.kept, bf16[512,128]{1,0:T(8,128)(2,1)S(1)} %collective-permute-done.2.left, bf16[512,128]{1,0:T(8,128)(2,1)S(1)} %collective-permute-done.3.right), custom_call_target="tpu_custom_call" | custom-call | tf_op jit(solution)/shard_map/gather/pallas_call | solution.py:331
Async XLA Ops:
  0.0 32.9 %copy-start = (s32[1,48]{1,0:T(1,128)S(1)}, s32[1,48]{1,0:T(1,128)}, u32[]{:S(2)}) copy-start(s32[1,48]{1,0:T(1,128)} %into.1) | copy-start | bytes 580
  0.0 11.8 %collective-permute-start.1 = (bf16[16,64,64]{2,1,0:T(8,128)(2,1)}, bf16[16,64,64]{2,1,0:T(8,128)(2,1)S(1)}, u32[]{:S(2)}, u32[]{:S(2)}) collective-permute-start(bf16[16,64,64]{2,1,0:T(8,128)(2,1)} %own.1), channel_id=1, source_target_pairs={{0,1},{1,2},{2,3},{3,4},{4,5},{5,6},{6,7},{7,8},{8,9},{9,10},{10,1... | collective-permute-start | bytes 393224 | tf_op jit(solution)/shard_map/ppermute | solution.py:36
  5.1 9.1 %collective-permute-start = (bf16[16,64,64]{2,1,0:T(8,128)(2,1)}, bf16[16,64,64]{2,1,0:T(8,128)(2,1)S(1)}, u32[]{:S(2)}, u32[]{:S(2)}) collective-permute-start(bf16[16,64,64]{2,1,0:T(8,128)(2,1)} %own.1), channel_id=1, source_target_pairs={{0,63},{1,0},{2,1},{3,2},{4,3},{5,4},{6,5},{7,6},{8,7},{9,8},{10,9... | collective-permute-start | bytes 393224 | tf_op jit(solution)/shard_map/ppermute | solution.py:36
  16.7 16.7 %collective-permute-start.2 = (bf16[512,128]{1,0:T(8,128)(2,1)S(1)}, bf16[512,128]{1,0:T(8,128)(2,1)S(1)}, u32[]{:S(2)}, u32[]{:S(2)}) collective-permute-start(bf16[512,128]{1,0:T(8,128)(2,1)S(1)} %get-tuple-element.23), channel_id=1, source_target_pairs={{0,64},{64,128},{128,192},{192,256},{256,320},{320,384},{384,448},... | collective-permute-start | bytes 393224 | tf_op jit(solution)/shard_map/ppermute | solution.py:36
  20.7 14.2 %collective-permute-start.3 = (bf16[512,128]{1,0:T(8,128)(2,1)S(1)}, bf16[512,128]{1,0:T(8,128)(2,1)S(1)}, u32[]{:S(2)}, u32[]{:S(2)}) collective-permute-start(bf16[512,128]{1,0:T(8,128)(2,1)S(1)} %get-tuple-element.24), channel_id=1, source_target_pairs={{0,704},{64,0},{128,64},{192,128},{256,192},{320,256},{384,320},{4... | collective-permute-start | bytes 393224 | tf_op jit(solution)/shard_map/ppermute | solution.py:36

commit v8 on v7

--- a/solution.py
+++ b/solution.py
@@ -163,7 +163,7 @@
 
 
 def far_kernel(
-    table, blocks, near_a, near_b, left, after, before, up, mid, down,
+    table, blocks, near_a, near_b, left, after, before, up, mid_a, mid_b, down,
     acc_a, acc_b, look, lows, highs, strip, sems,
 ):
     to_look = pltpu.make_async_copy(table, look, sems.at[0])
@@ -205,9 +205,12 @@
         return carry
 
     lax.fori_loop(0, ROWS, finish, 0, unroll=UNROLL_STRIP)
-    for n, out in enumerate((down, mid, up)):
+    for n, out in ((2, up), (0, down)):
         rows = slice(n * BUF * HALF, (n + 1) * BUF * HALF)
         out[...] = (acc_a[rows, :] + pltpu.roll(acc_b[rows, :], W, 1)).astype(out.dtype)
+    rows = slice(BUF * HALF, 2 * BUF * HALF)
+    mid_a[...] = acc_a[rows, :]
+    mid_b[...] = acc_b[rows, :]
 
 
 def by_tile(source, blocks):
@@ -218,7 +221,7 @@
     return jnp.concatenate(groups, axis=1)
 
 
-def route_kernel(into, mid, pick, kept):
+def route_kernel(into, mid_a, mid_b, pick, kept):
     chosen = jnp.broadcast_to(into[...], (8, 3 * BUF)).astype(F32).astype(BF)
 
     def one_hot(blocks, source):
@@ -234,7 +237,7 @@
 
     pick[...] = one_hot(2 * BUF, lambda block: jnp.where(block < BUF, block, block + BUF))
     own = one_hot(BUF, lambda block: block + BUF)
-    value = by_tile(mid, BUF)
+    value = by_tile(mid_a[...] + pltpu.roll(mid_b[...], W, 1), BUF)
     top = value.astype(BF)
     rest = value - top.astype(F32)
     middle = rest.astype(BF)
@@ -292,11 +295,12 @@
 
 def far(*operands):
     sent = jax.ShapeDtypeStruct(THIRD, BF)
+    own = jax.ShapeDtypeStruct(THIRD, F32)
     return pl.pallas_call(
         far_kernel,
-        out_shape=(sent, jax.ShapeDtypeStruct(THIRD, F32), sent),
+        out_shape=(sent, own, own, sent),
         in_specs=[VMEM] * 7,
-        out_specs=(VMEM,) * 3,
+        out_specs=(VMEM,) * 4,
         scratch_shapes=[
             pltpu.VMEM(SUMS.shape, F32),
             pltpu.VMEM(SUMS.shape, F32),
@@ -319,7 +323,7 @@
             jax.ShapeDtypeStruct((rows, 16 * BUF), BF),
             jax.ShapeDtypeStruct((rows, LANES * HALF // 8), F32),
         ),
-        in_specs=[VMEM, VMEM],
+        in_specs=[VMEM] * 3,
         out_specs=(VMEM, VMEM),
         compiler_params=pltpu.CompilerParams(vmem_limit_bytes=24 << 20),
         cost_estimate=pl.CostEstimate(flops=10**9, bytes_accessed=10**7, transcendentals=0),
@@ -342,10 +346,10 @@
     before = shifted(prolong, "inner", 1)
     after = shifted(prolong, "inner", -1)
     blocks, acc_a, acc_b, table, left = near(matrix_blocks, prolong, columns, partial_slot)
-    up, mid, down = far(table, blocks, acc_a, acc_b, left, after, before)
+    up, mid_a, mid_b, down = far(table, blocks, acc_a, acc_b, left, after, before)
     from_left = shifted(up, "slab", 1)
     from_right = shifted(down, "slab", -1)
-    pick, kept = route(into_slot, mid)
+    pick, kept = route(into_slot, mid_a, mid_b)
     return gather(pick, kept, from_left, from_right)
 
 

time: 36.1 us -> 36.1 us (level)
  no operation moved by 1% of the time
where the time goes in v8:
time: 36.1 us; the launch traced here: 35.8 us
  starting transfers between devices  23.3 us (65%)
  Pallas kernels  8.72 us (24%)
  waiting for transfers between devices  3.79 us (10%)
    ppermute x4, starting transfers between devices, shifted(): return lax.ppermute(value, axis, pairs)  23.3 us
    pallas_call x1, Pallas kernels, near(): pl.pallas_call(near_kernel, out_shape=(jax.ShapeDtypeStruct((DEPTH, 9 * W...  4.81 us
    ppermute x4, waiting for transfers between devices, shifted(): return lax.ppermute(value, axis, pairs)  3.79 us
    pallas_call x1, Pallas kernels, far(): pl.pallas_call(far_kernel, out_shape=(sent, own, own, sent), in_specs=[VM...  2.41 us
    pallas_call x1, Pallas kernels, gather(): pl.pallas_call(gather_kernel, out_shape=jax.ShapeDtypeStruct((SLOTS, W *...  1.03 us
  transfers between devices with their start and end apart: 4, of which 2 were waited for; matrix products, arithmetic and copies ran while one was open for 0% of the time, Pallas kernels for 15%

profile of v8, /device:TPU:25, one launch (start us, length us, event | category | flops | bytes accessed | tf_op | source)
XLA Modules:
  0.0 35.8 jit_solution(7494311709462428520)
XLA Ops:
  0.0 0.0 copy-start
  0.0 5.1 %collective-permute-start.1 = (bf16[16,64,64]{2,1,0:T(8,128)(2,1)}, bf16[16,64,64]{2,1,0:T(8,128)(2,1)S(1)}, u32[]{:S(2)}, u32[]{:S(2)}) collective-permute-start(bf16[16,64,64]{2,1,0:T(8,128)(2,1)} %own.1), channel_id=1, source_target_pairs={{0,1},{1,2},{2,3},{3,4},{4,5},{5,6},{6,7},{7,8},{8,9},{9,10},{10,1... | collective-permute-start | bytes 393224 | tf_op jit(solution)/shard_map/ppermute | solution.py:36
  5.1 1.9 %collective-permute-start = (bf16[16,64,64]{2,1,0:T(8,128)(2,1)}, bf16[16,64,64]{2,1,0:T(8,128)(2,1)S(1)}, u32[]{:S(2)}, u32[]{:S(2)}) collective-permute-start(bf16[16,64,64]{2,1,0:T(8,128)(2,1)} %own.1), channel_id=1, source_target_pairs={{0,63},{1,0},{2,1},{3,2},{4,3},{5,4},{6,5},{7,6},{8,7},{9,8},{10,9... | collective-permute-start | bytes 393224 | tf_op jit(solution)/shard_map/ppermute | solution.py:36
  7.0 4.8 %near.1 = (bf16[8,576,256]{2,1,0:T(8,128)(2,1)S(1)}, f32[1536,128]{1,0:T(8,128)S(1)}, f32[1536,128]{1,0:T(8,128)S(1)}, s32[16,27]{1,0:T(8,128)S(1)}, bf16[16,64,64]{2,1,0:T(8,128)(2,1)S(1)}) custom-call(bf16[16,27,64,64]{3,2,1,0:T(8,128)(2,1)} %blocks.1, bf16[16,64,64]{2,1,0:T(8,128)(2,1)} %own.1, s32[16,27]{1,0:T(8,128)} %cols.1, s32[16,27]{1,0:T(8,128)} %slots.1), custom_call_target="tpu_custom_call" | custom-call | flops 1000000000 | bytes 12000000 | tf_op jit(solution)/shard_map/near/pallas_call | solution.py:268
  11.9 0.0 collective-permute-done.1.before
  11.9 2.4 %collective-permute-done.after = bf16[16,64,64]{2,1,0:T(8,128)(2,1)S(1)} collective-permute-done((bf16[16,64,64]{2,1,0:T(8,128)(2,1)}, bf16[16,64,64]{2,1,0:T(8,128)(2,1)S(1)}, u32[]{:S(2)}, u32[]{:S(2)}) %collective-permute-start) | collective-permute-done | bytes 131104 | tf_op jit(solution)/shard_map/ppermute | solution.py:36
  14.2 2.4 %far.1 = (bf16[512,128]{1,0:T(8,128)(2,1)S(1)}, f32[512,128]{1,0:T(8,128)S(1)}, f32[512,128]{1,0:T(8,128)S(1)}, bf16[512,128]{1,0:T(8,128)(2,1)S(1)}) custom-call(s32[16,27]{1,0:T(8,128)S(1)} %get-tuple-element.16.table, bf16[8,576,256]{2,1,0:T(8,128)(2,1)S(1)} %get-tuple-element.17.blocks, f32[1536,128]{1,0:T(8,128)S(1)} %get-tuple-element.18.near_a, ...), custom_call_target="tpu_custom_call" | custom-call | tf_op jit(solution)/shard_map/far/pallas_call | solution.py:299
  16.6 4.0 %collective-permute-start.2 = (bf16[512,128]{1,0:T(8,128)(2,1)S(1)}, bf16[512,128]{1,0:T(8,128)(2,1)S(1)}, u32[]{:S(2)}, u32[]{:S(2)}) collective-permute-start(bf16[512,128]{1,0:T(8,128)(2,1)S(1)} %get-tuple-element.25), channel_id=1, source_target_pairs={{0,64},{64,128},{128,192},{192,256},{256,320},{320,384},{384,448},... | collective-permute-start | bytes 393224 | tf_op jit(solution)/shard_map/ppermute | solution.py:36
  20.7 12.2 %collective-permute-start.3 = (bf16[512,128]{1,0:T(8,128)(2,1)S(1)}, bf16[512,128]{1,0:T(8,128)(2,1)S(1)}, u32[]{:S(2)}, u32[]{:S(2)}) collective-permute-start(bf16[512,128]{1,0:T(8,128)(2,1)S(1)} %get-tuple-element.26), channel_id=1, source_target_pairs={{0,704},{64,0},{128,64},{192,128},{256,192},{320,256},{384,320},{4... | collective-permute-start | bytes 393224 | tf_op jit(solution)/shard_map/ppermute | solution.py:36
  32.9 0.0 copy-done
  32.9 0.5 %route.1 = (bf16[256,256]{1,0:T(8,128)(2,1)S(1)}, f32[256,512]{1,0:T(8,128)S(1)}) custom-call(s32[1,48]{1,0:T(1,128)S(1)} %copy-done, f32[512,128]{1,0:T(8,128)S(1)} %get-tuple-element.21.mid_a, f32[512,128]{1,0:T(8,128)S(1)} %get-tuple-element.22.mid_b), custom_call_target="tpu_custom_call" | custom-call | flops 1000000000 | bytes 10000000 | tf_op jit(solution)/shard_map/route/pallas_call | solution.py:320
  33.4 0.0 collective-permute-done.2.left
  33.4 1.4 %collective-permute-done.3.right = bf16[512,128]{1,0:T(8,128)(2,1)S(1)} collective-permute-done((bf16[512,128]{1,0:T(8,128)(2,1)S(1)}, bf16[512,128]{1,0:T(8,128)(2,1)S(1)}, u32[]{:S(2)}, u32[]{:S(2)}) %collective-permute-start.3) | collective-permute-done | bytes 131104 | tf_op jit(solution)/shard_map/ppermute | solution.py:36
  34.8 1.0 %gather.1 = f32[32,4096]{1,0:T(8,128)} custom-call(bf16[256,256]{1,0:T(8,128)(2,1)S(1)} %get-tuple-element.23.pick, f32[256,512]{1,0:T(8,128)S(1)} %get-tuple-element.24.kept, bf16[512,128]{1,0:T(8,128)(2,1)S(1)} %collective-permute-done.2.left, bf16[512,128]{1,0:T(8,128)(2,1)S(1)} %collective-permute-done.3.right), custom_call_target="tpu_custom_call" | custom-call | tf_op jit(solution)/shard_map/gather/pallas_call | solution.py:335
Async XLA Ops:
  0.0 32.9 %copy-start = (s32[1,48]{1,0:T(1,128)S(1)}, s32[1,48]{1,0:T(1,128)}, u32[]{:S(2)}) copy-start(s32[1,48]{1,0:T(1,128)} %into.1) | copy-start | bytes 580
  0.0 11.9 %collective-permute-start.1 = (bf16[16,64,64]{2,1,0:T(8,128)(2,1)}, bf16[16,64,64]{2,1,0:T(8,128)(2,1)S(1)}, u32[]{:S(2)}, u32[]{:S(2)}) collective-permute-start(bf16[16,64,64]{2,1,0:T(8,128)(2,1)} %own.1), channel_id=1, source_target_pairs={{0,1},{1,2},{2,3},{3,4},{4,5},{5,6},{6,7},{7,8},{8,9},{9,10},{10,1... | collective-permute-start | bytes 393224 | tf_op jit(solution)/shard_map/ppermute | solution.py:36
  5.1 9.1 %collective-permute-start = (bf16[16,64,64]{2,1,0:T(8,128)(2,1)}, bf16[16,64,64]{2,1,0:T(8,128)(2,1)S(1)}, u32[]{:S(2)}, u32[]{:S(2)}) collective-permute-start(bf16[16,64,64]{2,1,0:T(8,128)(2,1)} %own.1), channel_id=1, source_target_pairs={{0,63},{1,0},{2,1},{3,2},{4,3},{5,4},{6,5},{7,6},{8,7},{9,8},{10,9... | collective-permute-start | bytes 393224 | tf_op jit(solution)/shard_map/ppermute | solution.py:36
  16.6 16.7 %collective-permute-start.2 = (bf16[512,128]{1,0:T(8,128)(2,1)S(1)}, bf16[512,128]{1,0:T(8,128)(2,1)S(1)}, u32[]{:S(2)}, u32[]{:S(2)}) collective-permute-start(bf16[512,128]{1,0:T(8,128)(2,1)S(1)} %get-tuple-element.25), channel_id=1, source_target_pairs={{0,64},{64,128},{128,192},{192,256},{256,320},{320,384},{384,448},... | collective-permute-start | bytes 393224 | tf_op jit(solution)/shard_map/ppermute | solution.py:36
  20.7 14.2 %collective-permute-start.3 = (bf16[512,128]{1,0:T(8,128)(2,1)S(1)}, bf16[512,128]{1,0:T(8,128)(2,1)S(1)}, u32[]{:S(2)}, u32[]{:S(2)}) collective-permute-start(bf16[512,128]{1,0:T(8,128)(2,1)S(1)} %get-tuple-element.26), channel_id=1, source_target_pairs={{0,704},{64,0},{128,64},{192,128},{256,192},{320,256},{384,320},{4... | collective-permute-start | bytes 393224 | tf_op jit(solution)/shard_map/ppermute | solution.py:36
